TPU v7x, 32 devices: a whole 2x2x4 slice. The times are simulated.
32 devices in a mesh: groups: 2 (over x), rows: 16 (over z, y, core).
Axes of the slice: x: 2, y: 2, z: 4, core: 2. Of those that a mesh axis runs over, the one named last changes fastest.
Arguments:
- block_input: bfloat16 [512, 352, 512], P(('groups', 'rows')), parts along dimension 0, may hold values from -6 to 6
- first_pre: bfloat16 [512, 352, 128], P(('groups', 'rows')), parts along dimension 0, may hold values from -6 to 6
- second_pre: bfloat16 [512, 352, 128], P(('groups', 'rows')), parts along dimension 0, may hold values from -6 to 6
- output_pre: bfloat16 [512, 352, 512], P(('groups', 'rows')), parts along dimension 0, may hold values from -6 to 6
- output_grad: bfloat16 [512, 352, 512], P('groups', None, 'rows'), parts along dimension 0, may hold values from -6 to 6
- first_weight: bfloat16 [512, 128], replicated, may hold values from -0.25 to 0.25
- middle_weight: bfloat16 [3, 3, 128, 128], replicated, may hold values from -0.1875 to 0.1875
- last_weight: bfloat16 [128, 512], replicated, may hold values from -0.5 to 0.5
Outputs:
- input_grad: bfloat16 [512, 352, 512], P(('groups', 'rows')), parts along dimension 0
- first_weight_grad: float32 [1024, 128], P(('groups', 'rows')), parts along dimension 0
- middle_weight_grad: float32 [6, 3, 128, 128], P('groups'), parts along dimension 0
- last_weight_grad: float32 [256, 512], P('groups'), parts along dimension 0
There are 2 independent parts, one for each index of `groups`. A program takes and returns all parts, laid end to end along the dimension named above; an argument that names none is the same for every part. Nothing has to cross between parts.
All inputs are finite; a program needn't handle non-finite values.
Results may differ from a plain program's by a relative error of at most 0.0049.
Values may be sent and summed in bfloat16 or wider, within the bound.
No kernel may reach another device: no remote copies, remote signals or barrier semaphores. Data moves between devices by JAX's collectives and lax.ppermute only.
A program may use at most 128 MiB of HBM per device.

v0:
```python
import math

import jax
import jax.numpy as jnp
from jax import lax
from jax.sharding import PartitionSpec as P


def with_halo(value, sides, width):
    for axis, dim in sides:
        size, length = (lax.axis_size(axis), value.shape[dim])
        up = [(i, (i + 1) % size) for i in range(size - 1)]
        down = [(j, i) for i, j in up]
        last = lax.slice_in_dim(value, length - width, length, axis=dim)
        leading = lax.slice_in_dim(value, 0, width, axis=dim)
        before = lax.ppermute(last, axis, up)
        after = lax.ppermute(leading, axis, down)
        value = jnp.concatenate([before, value, after], axis=dim)
    return value


def contract_rows(left, right):
    return lax.dot_general(
        left, right, (((0,), (0,)), ((), ())), preferred_element_type=jnp.float32
    )


def shards(
    block_input,
    first_pre,
    second_pre,
    output_pre,
    output_grad,
    first_weight,
    middle_weight,
    last_weight,
):
    tile_rows, map_cols, channels = block_input.shape
    inner_width = first_pre.shape[2]
    pixels = tile_rows * map_cols
    factor = 1.0 / math.sqrt(pixels * lax.axis_size("rows"))
    spatial = lax.all_to_all(output_grad, "rows", split_axis=0, concat_axis=2, tiled=True)
    masked_out = jnp.where(output_pre > 0, spatial, jnp.zeros_like(spatial))
    second_act = jnp.maximum(second_pre, jnp.zeros_like(second_pre))
    first_act = jnp.maximum(first_pre, jnp.zeros_like(first_pre))
    out_flat = masked_out.reshape(pixels, channels)
    last_part = contract_rows(second_act.reshape(pixels, inner_width), out_flat)
    last_total = lax.psum(last_part, "rows")
    inner = lax.dot_general(
        out_flat, last_weight, (((1,), (1,)), ((), ())), preferred_element_type=jnp.float32
    )
    second_grad = jnp.where(second_pre.reshape(pixels, inner_width) > 0, inner, 0.0).astype(
        jnp.bfloat16
    )
    second_flat = second_grad
    second_grad = second_flat.reshape(tile_rows, map_cols, inner_width)
    act_ext = with_halo(first_act, (("rows", 0),), 1)
    act_padded = jnp.pad(act_ext, ((0, 0), (1, 1), (0, 0)))
    taps = []
    for row_tap in range(3):
        line = []
        for col_tap in range(3):
            window = act_padded[
                row_tap : row_tap + tile_rows, col_tap : col_tap + map_cols
            ].reshape(pixels, inner_width)
            line.append(contract_rows(window, second_flat))
        taps.append(jnp.stack(line))
    middle_part = jnp.stack(taps)
    grad_ext = with_halo(second_grad, (("rows", 0),), 1)
    grad_padded = jnp.pad(grad_ext, ((0, 0), (1, 1), (0, 0)))
    total = jnp.zeros((pixels, inner_width), jnp.float32)
    for row_tap in range(3):
        for col_tap in range(3):
            moved = grad_padded[
                2 - row_tap : 2 - row_tap + tile_rows, 2 - col_tap : 2 - col_tap + map_cols
            ].reshape(pixels, inner_width)
            total = total + lax.dot_general(
                moved,
                middle_weight[row_tap, col_tap],
                (((1,), (1,)), ((), ())),
                preferred_element_type=jnp.float32,
            )
    first_grad = jnp.where(first_pre.reshape(pixels, inner_width) > 0, total, 0.0).astype(
        jnp.bfloat16
    )
    input_flat = block_input.reshape(pixels, channels)
    first_wgrad = (
        lax.psum_scatter(
            contract_rows(input_flat, first_grad), "rows", scatter_dimension=0, tiled=True
        )
        * factor
    )
    back = lax.dot_general(
        first_grad, first_weight, (((1,), (1,)), ((), ())), preferred_element_type=jnp.float32
    )
    input_grad = (
        (back + out_flat.astype(jnp.float32))
        .astype(jnp.bfloat16)
        .reshape(tile_rows, map_cols, channels)
    )
    middle_total = lax.psum(middle_part, "rows")
    return (input_grad, first_wgrad, middle_total * factor, last_total * factor)


def solution(mesh):
    placed = (
        P(("groups", "rows"), None, None),
        P(("groups", "rows"), None, None),
        P(("groups", "rows"), None, None),
        P(("groups", "rows"), None, None),
        P("groups", None, "rows"),
        P(),
        P(),
        P(),
    )
    return jax.shard_map(
        shards,
        mesh=mesh,
        in_specs=placed,
        out_specs=(
            P(("groups", "rows"), None, None),
            P(("groups", "rows"), None),
            P("groups", None, None, None),
            P("groups", None),
        ),
        check_vma=False,
    )
```

profile of v0, /device:TPU:0, one launch (start us, length us, event | category | flops | bytes accessed | tf_op | source)
XLA Modules:
  0.0 376.6 jit_solution(985985323894171516)
XLA Ops:
  7.2 9.7 %copy.21 = bf16[256,352,32]{1,2,0:T(8,128)(2,1)} copy(bf16[256,352,32]{0,2,1:T(8,128)(2,1)} %param.12) | data formatting | bytes 11534336 | tf_op args[4]
  16.8 7.6 %all-to-all-start = ((bf16[256,352,32]{1,2,0:T(8,128)(2,1)}), bf16[256,352,32]{1,2,0:T(8,128)(2,1)}, u32[]{:S(2)}, u32[]{:S(2)}) async-start(bf16[256,352,32]{1,2,0:T(8,128)(2,1)} %copy.21), calls=%async_computation | async-start | bytes 12582912 | tf_op jit(solution)/shard_map/all_to_all | solution.py:42
  24.6 2.4 collective-permute-start.2
  27.0 1.3 collective-permute-start.3
  28.3 1.3 broadcast_compare_fusion.1
  29.6 1.3 broadcast_compare_fusion
  30.9 8.3 %copy.20 = bf16[16,352,512]{1,2,0:T(8,128)(2,1)} copy(bf16[16,352,512]{2,1,0:T(8,128)(2,1)} %param.11) | data formatting | bytes 11534336 | tf_op args[3]
  39.2 1.7 pad_maximum_fusion.1
  41.4 3.9 %fusion.33 = (bf16[16,352,128]{2,1,0:T(8,128)(2,1)}, bf16[16,352,128]{2,1,0:T(8,128)(2,1)}, bf16[16,352,128]{2,1,0:T(8,128)(2,1)}, bf16[16,352,128]{2,1,0:T(8,12...) fusion(bf16[18,354,128]{2,1,0:T(8,128)(2,1)S(1)} %select_maximum_fusion), kind=kLoop, calls=%fused_computation.73 | loop fusion | bytes 17301504 | tf_op jit(solution)/shard_map/slice | solution.py:63
  45.3 93.3 %all-to-all-done = bf16[256,352,32]{1,2,0:T(8,128)(2,1)} async-done(((bf16[256,352,32]{1,2,0:T(8,128)(2,1)}), bf16[256,352,32]{1,2,0:T(8,128)(2,1)}, u32[]{:S(2)}, u32[]{:S(2)}) %all-to-all-start) | async-done | bytes 5767200 | tf_op jit(solution)/shard_map/all_to_all | solution.py:42
  138.6 6.4 %copy.22 = bf16[16,352,16,32]{1,3,2,0:T(8,128)(2,1)} copy(bf16[16,352,16,32]{1,3,0,2:T(8,128)(2,1)} %bitcast.3) | data formatting | bytes 11534336 | tf_op jit(solution)/shard_map/all_to_all | solution.py:42
  145.0 8.0 %compare_select_fusion = bf16[16,352,512]{1,2,0:T(8,128)(2,1)} fusion(bf16[16,352,512]{1,2,0:T(8,128)(2,1)} %copy.20, bf16[16,352,16,32]{1,3,2,0:T(8,128)(2,1)} %copy.22), kind=kLoop, calls=%fused_computation | loop fusion | flops 5767168 | bytes 17301504 | tf_op jit(solution)/shard_map/jit(_where)/select_n | solution.py:43
  153.1 8.5 %copy.23 = bf16[16,352,512]{2,1,0:T(8,128)(2,1)} copy(bf16[16,352,512]{1,2,0:T(8,128)(2,1)} %compare_select_fusion) | data formatting | bytes 11534336 | tf_op jit(solution)/shard_map/jit(_where)/select_n | solution.py:43
  161.6 5.8 %fusion.8 = f32[128,512]{1,0:T(8,128)} fusion(bf16[16,352,512]{1,2,0:T(8,128)(2,1)} %compare_select_fusion, bf16[16,352,128]{2,1,0:T(8,128)(2,1)S(1)} %copy-done.12), kind=kOutput, calls=%fused_computation.28 | convolution fusion | flops 738918400 | bytes 7471104 | tf_op jit(solution)/shard_map/dot_general | solution.py:23
  167.5 1.7 fusion.3
  179.9 2.7 collective-permute-start
  182.6 1.3 collective-permute-start.1
  185.0 8.5 %collective-permute-done.1 = bf16[1,352,128]{2,1,0:T(8,128)(2,1)S(1)} collective-permute-done((bf16[1,352,128]{2,1,0:T(8,128)(2,1)S(1)}, bf16[1,352,128]{2,1,0:T(8,128)(2,1)S(1)}, u32[]{:S(2)}, u32[]{:S(2)}) %collective-permute-start.1) | collective-permute-done | bytes 90144 | tf_op jit(solution)/shard_map/ppermute | solution.py:17
  194.1 2.4 fusion.34
  205.5 6.8 %add_convert_fusion = bf16[5632,512]{1,0:T(8,128)(2,1)} fusion(bf16[5632,512]{1,0:T(8,128)(2,1)} %bitcast.124, bf16[5632,128]{1,0:T(8,128)(2,1)S(1)} %fusion.2, bf16[512,128]{1,0:T(8,128)(2,1)S(1)} %copy-done), kind=kOutput, calls=%fused_computation.1 | convolution fusion | flops 746848256 | bytes 13107200 | tf_op jit(solution)/shard_map/dot_general | solution.py:93
  212.3 97.3 %all-reduce.5.cloned.1.call-done = (f32[3,3,128,128]{3,2,1,0:T(8,128)}, f32[128,512]{1,0:T(8,128)}) async-done(((f32[3,3,128,128]{3,2,1,0:T(8,128)}, f32[128,512]{1,0:T(8,128)}), (f32[3,3,128,128]{3,2,1,0:T(8,128)}, f32[128,512]{1,0:T(8,128)})) %all-reduce.5.cloned.1.call-update) | async-done | bytes 851984 | tf_op jit(solution)/shard_map/psum | solution.py:101
  309.6 1.7 broadcast_multiply_fusion.1
  311.3 1.9 broadcast_multiply_fusion
  313.2 55.1 %reduce-scatter.4.cloned.1.call-done = f32[32,128]{1,0:T(8,128)} async-done(((f32[512,128]{1,0:T(8,128)}), f32[32,128]{1,0:T(8,128)}) %reduce-scatter.4.cloned.1.call-update) | async-done | bytes 16400
  (78 shorter events, 23.3 us)
Async XLA Ops:
  7.2 198.3 %copy-start = (bf16[512,128]{1,0:T(8,128)(2,1)S(1)}, bf16[512,128]{1,0:T(8,128)(2,1)}, u32[]{:S(2)}) copy-start(bf16[512,128]{1,0:T(8,128)(2,1)} %param.13) | copy-start | bytes 393220
  16.8 7.6 %copy-start.2 = (bf16[16,352,128]{2,1,0:T(8,128)(2,1)S(1)}, bf16[16,352,128]{2,1,0:T(8,128)(2,1)}, u32[]{:S(2)}) copy-start(bf16[16,352,128]{2,1,0:T(8,128)(2,1)} %param.9) | copy-start | bytes 4325380
  16.8 121.8 %all-to-all-start = ((bf16[256,352,32]{1,2,0:T(8,128)(2,1)}), bf16[256,352,32]{1,2,0:T(8,128)(2,1)}, u32[]{:S(2)}, u32[]{:S(2)}) async-start(bf16[256,352,32]{1,2,0:T(8,128)(2,1)} %copy.21), calls=%async_computation | async-start | bytes 12582912 | tf_op jit(solution)/shard_map/all_to_all | solution.py:42
  24.4 285.2 %all-reduce.5.cloned.1.call-start = ((), (), s32[]{:S(2)}) async-start(), calls=%async_computation.3 | async-start | bytes 1703936 | tf_op jit(solution)/shard_map/psum | solution.py:101
  24.6 5.0 %copy-start.11 = (bf16[16,352,128]{2,1,0:T(8,128)(2,1)S(1)}, bf16[16,352,128]{2,1,0:T(8,128)(2,1)}, u32[]{:S(2)}) copy-start(bf16[16,352,128]{2,1,0:T(8,128)(2,1)} %param.10) | copy-start | bytes 4325380
  24.6 14.6 %collective-permute-start.2 = (bf16[1,352,128]{2,1,0:T(8,128)(2,1)S(1)}, bf16[1,352,128]{2,1,0:T(8,128)(2,1)S(1)}, u32[]{:S(2)}, u32[]{:S(2)}) collective-permute-start(bf16[1,352,128]{2,1,0:T(8,128)(2,1)S(1)} %get-tuple-element.32), channel_id=1, source_target_pairs={{0,1},{1,2},{2,3},{3,4},{4,5},{5,6},{6,7},{7,8},{8,9},{9,10},{10,1... | collective-permute-start | bytes 270344 | tf_op jit(solution)/shard_map/ppermute | solution.py:16
  27.0 12.2 %collective-permute-start.3 = (bf16[1,352,128]{2,1,0:T(8,128)(2,1)S(1)}, bf16[1,352,128]{2,1,0:T(8,128)(2,1)S(1)}, u32[]{:S(2)}, u32[]{:S(2)}) collective-permute-start(bf16[1,352,128]{2,1,0:T(8,128)(2,1)S(1)} %get-tuple-element.33), channel_id=1, source_target_pairs={{1,0},{2,1},{3,2},{4,3},{5,4},{6,5},{7,6},{8,7},{9,8},{10,9},{11,1... | collective-permute-start | bytes 270344 | tf_op jit(solution)/shard_map/ppermute | solution.py:17
  153.1 8.5 %copy-start.12 = (bf16[16,352,128]{2,1,0:T(8,128)(2,1)S(1)}, bf16[16,352,128]{2,1,0:T(8,128)(2,1)}, u32[]{:S(2)}) copy-start(bf16[16,352,128]{2,1,0:T(8,128)(2,1)} %param.10) | copy-start | bytes 4325380
  161.6 5.8 %copy-start.1 = (bf16[16,352,512]{2,1,0:T(8,128)(2,1)S(1)}, bf16[16,352,512]{2,1,0:T(8,128)(2,1)}, u32[]{:S(2)}) copy-start(bf16[16,352,512]{2,1,0:T(8,128)(2,1)} %copy.23) | copy-start | bytes 17301508
  161.6 5.8 %copy-start.14 = (pred[16,352,128]{2,1,0:T(32,128)(4,1)S(1)}, pred[16,352,128]{2,1,0:T(32,128)(4,1)}, u32[]{:S(2)}) copy-start(pred[16,352,128]{2,1,0:T(32,128)(4,1)} %broadcast_compare_fusion) | copy-start | bytes 2162692
  161.6 5.8 %copy-start.16 = (bf16[128,512]{1,0:T(8,128)(2,1)S(1)}, bf16[128,512]{1,0:T(8,128)(2,1)}, u32[]{:S(2)}) copy-start(bf16[128,512]{1,0:T(8,128)(2,1)} %param.15) | copy-start | bytes 393220
  167.5 1.7 copy-start.10
  169.2 1.4 copy-start.9
  170.5 1.4 copy-start.8
  171.9 1.4 copy-start.7
  173.3 1.4 copy-start.4
  175.2 1.4 copy-start.6
  177.9 1.4 copy-start.3
  179.9 5.2 %collective-permute-start = (bf16[1,352,128]{2,1,0:T(8,128)(2,1)S(1)}, bf16[1,352,128]{2,1,0:T(8,128)(2,1)S(1)}, u32[]{:S(2)}, u32[]{:S(2)}) collective-permute-start(bf16[1,352,128]{2,1,0:T(8,128)(2,1)S(1)} %get-tuple-element.36), channel_id=1, source_target_pairs={{0,1},{1,2},{2,3},{3,4},{4,5},{5,6},{6,7},{7,8},{8,9},{9,10},{10,1... | collective-permute-start | bytes 270344 | tf_op jit(solution)/shard_map/ppermute | solution.py:16
  182.6 11.0 %collective-permute-start.1 = (bf16[1,352,128]{2,1,0:T(8,128)(2,1)S(1)}, bf16[1,352,128]{2,1,0:T(8,128)(2,1)S(1)}, u32[]{:S(2)}, u32[]{:S(2)}) collective-permute-start(bf16[1,352,128]{2,1,0:T(8,128)(2,1)S(1)} %get-tuple-element.37), channel_id=1, source_target_pairs={{1,0},{2,1},{3,2},{4,3},{5,4},{6,5},{7,6},{8,7},{9,8},{10,9},{11,1... | collective-permute-start | bytes 270344 | tf_op jit(solution)/shard_map/ppermute | solution.py:17
  184.8 183.4 %reduce-scatter.4.cloned.1.call-start = ((), (), s32[]{:S(2)}) async-start(), calls=%async_computation.2 | async-start | bytes 278528
  194.1 2.4 copy-start.15
  200.5 2.4 slice-start
  201.6 2.0 slice-start.1
  (2 other events, 2.5 us)
Sparse Core Ops, SparseCore 0:
  184.9 124.6 all-reduce.4
  313.1 55.1 reduce-scatter.3
where the time goes:
time: 378 us; the launch traced here: 377 us
  waiting for transfers between devices  254 us (67%)
  local copies, waits for them, and re-layouts  48.8 us (13%)
  matrix products  25.6 us (7%)
  other arithmetic  18 us (5%)
  starting transfers between devices  15.5 us (4%)
  between operations  14.4 us (4%)
    psum x1, waiting for transfers between devices, shards(): middle_total = lax.psum(middle_part, 'rows')  97.3 us
    all_to_all x1, waiting for transfers between devices, shards(): lax.all_to_all(output_grad, 'rows', split_axis=0, concat_axis=2, tiled=True)  93.3 us
    unnamed x3, waiting for transfers between devices  55.1 us
    unnamed x43, local copies, waits for them, and re-layouts  27.6 us
    dot_general x11, matrix products, contract_rows(): lax.dot_general(left, right, (((0,), (0,)), ((), ())), preferred_element_...  12 us
    ppermute x2, waiting for transfers between devices, with_halo(): after = lax.ppermute(leading, axis, down)  8.54 us
    select_n x1, local copies, waits for them, and re-layouts, shards(): masked_out = jnp.where(output_pre > 0, spatial, jnp.zeros_like(spatial))  8.53 us
    select_n x1, other arithmetic, shards(): masked_out = jnp.where(output_pre > 0, spatial, jnp.zeros_like(spatial))  8.04 us
  transfers between devices with their start and end apart: 7, of which 4 were waited for; matrix products, arithmetic and copies ran while one was open for 10% of the time, Pallas kernels for 0%

commit v1 on v0

v1 whole, which is shorter than its diff:
```python
import functools
import math

import jax
import jax.numpy as jnp
from jax import lax
from jax.experimental import pallas as pl
from jax.experimental.pallas import tpu as pltpu
from jax.sharding import PartitionSpec as P

BF = jnp.bfloat16
F32 = jnp.float32
AXIS = "rows"
BLK = 16
LANES = 128


def dims(lhs, rhs):
    return (((lhs,), (rhs,)), ((), ()))


def mm(a, b):
    return lax.dot_general(a, b, dims(1, 0), preferred_element_type=F32)


def mm_nt(a, b):
    return lax.dot_general(a, b, dims(1, 1), preferred_element_type=F32)


def unit(count, offset, cap):
    return max(u for u in range(1, cap + 1) if count % u == 0 and offset % u == 0)


def params():
    return pltpu.CompilerParams(
        dimension_semantics=("arbitrary",), vmem_limit_bytes=48 * 2**20
    )


def cost(flops, nbytes):
    return pl.CostEstimate(flops=int(flops), transcendentals=0, bytes_accessed=int(nbytes))


def whole(shape):
    zeros = (0,) * len(shape)
    return pl.BlockSpec(shape, lambda i: zeros)


def eye(size):
    a = lax.broadcasted_iota(jnp.int32, (size, size), 0)
    b = lax.broadcasted_iota(jnp.int32, (size, size), 1)
    return (a == b).astype(BF)


def pack_kernel(tile_rows, units, groups, x_ref, eye_ref, out_ref):
    side = eye_ref.shape[0]
    per = side // tile_rows
    depth = groups * LANES
    for u in range(units):
        for h in range(x_ref.shape[1] // side):
            part = x_ref[u * depth : (u + 1) * depth, h * side : (h + 1) * side]
            turned = mm_nt(eye_ref[...], part).astype(BF)
            for g in range(groups):
                piece = turned[:, g * LANES : (g + 1) * LANES]
                out_ref[
                    h * per : (h + 1) * per, u, g * tile_rows : (g + 1) * tile_rows, :
                ] = piece.reshape(per, tile_rows, LANES)


def pack(x, count, tile_rows, groups, start, blocks):
    depth = groups * LANES
    height = x.shape[1]
    side = 256 if height % 256 == 0 else LANES
    u = unit(blocks, start, 4)
    first = start // u
    return pl.pallas_call(
        functools.partial(pack_kernel, tile_rows, u, groups),
        grid=(blocks // u,),
        in_specs=[
            pl.BlockSpec((u * depth, height), lambda i: (first + i, 0)),
            whole((side, side)),
        ],
        out_specs=pl.BlockSpec(
            (count, u, groups * tile_rows, LANES), lambda i: (0, i, 0, 0)
        ),
        out_shape=jax.ShapeDtypeStruct((count, blocks, groups * tile_rows, LANES), BF),
        compiler_params=params(),
        cost_estimate=cost(
            2 * height * side * blocks * depth, 4 * blocks * depth * height
        ),
        name="pack",
    )(x, eye(side))


def open_kernel(units, join, alias, *refs):
    if alias:
        refs = refs[1:]
    (recv, opre, spre, lanes_ref, pixels_ref, weight, lw_in, buf, sg, lw) = refs
    rows = opre.shape[0]
    tiles = recv.shape[0] // join
    height = recv.shape[2]
    pixels = rows * BLK

    @pl.when(pl.program_id(0) == 0)
    def _():
        lw[...] = lw_in[...]

    for u in range(units):
        stack = jnp.concatenate(
            [
                jnp.concatenate([recv[t * join + s, u] for s in range(join)], axis=1)
                for t in range(tiles)
            ],
            axis=0,
        )
        sorted_lanes = mm(stack, lanes_ref[...]).astype(BF)
        by_pixel = jnp.concatenate(
            [
                jnp.concatenate(
                    [
                        sorted_lanes[
                            t * height : (t + 1) * height, j * LANES : (j + 1) * LANES
                        ]
                        for t in range(tiles)
                    ],
                    axis=1,
                )
                for j in range(join)
            ],
            axis=0,
        )
        spatial = mm(pixels_ref[...], by_pixel)
        cols = slice(u * BLK, (u + 1) * BLK)
        gate = opre[:, cols, :].reshape(pixels, tiles * LANES).astype(F32) > 0
        masked = jnp.where(gate, spatial, 0.0).astype(BF)
        buf[:, cols, :] = masked.reshape(rows, BLK, tiles * LANES)
        pre = spre[:, cols, :].reshape(pixels, LANES).astype(F32)
        inner = mm_nt(masked, weight[...])
        sg[:, cols, :] = (
            jnp.where(pre > 0, inner, 0.0).astype(BF).reshape(rows, BLK, LANES)
        )
        act = jnp.maximum(pre, 0.0).astype(BF)
        part = mm(jnp.transpose(act), masked)
        for t in range(tiles):
            lw[t] += part[:, t * LANES : (t + 1) * LANES]


def open_block(buf, recv, opre, spre, lane_sort, pixel_sort, weight, lw_in, join, start):
    rows, _, channels = opre.shape
    count, blocks, height, _ = recv.shape
    tiles = channels // LANES
    u = unit(blocks, start, 2)
    first = start // u
    alias = buf is not None
    wide = lambda c: pl.BlockSpec((rows, u * BLK, c), lambda i: (0, first + i, 0))
    pixels = rows * BLK * blocks
    call = pl.pallas_call(
        functools.partial(open_kernel, u, join, alias),
        grid=(blocks // u,),
        in_specs=([pl.BlockSpec(memory_space=pl.ANY)] if alias else [])
        + [
            pl.BlockSpec((count, u, height, LANES), lambda i: (0, i, 0, 0)),
            wide(channels),
            wide(LANES),
            whole(lane_sort.shape),
            whole(pixel_sort.shape),
            whole(weight.shape),
            whole(lw_in.shape),
        ],
        out_specs=[
            wide(channels),
            pl.BlockSpec((rows, u * BLK, LANES), lambda i: (0, i, 0)),
            whole(lw_in.shape),
        ],
        out_shape=[
            jax.ShapeDtypeStruct(opre.shape, BF),
            jax.ShapeDtypeStruct((rows, blocks * BLK, LANES), BF),
            jax.ShapeDtypeStruct(lw_in.shape, F32),
        ],
        input_output_aliases={0: 0} if alias else {},
        compiler_params=params(),
        cost_estimate=cost(
            2 * pixels * channels * (512 + 256 + 256), 2 * pixels * (3 * channels + 256)
        ),
        name="open_block",
    )
    args = (recv, opre, spre, lane_sort, pixel_sort, weight, lw_in)
    return call(*(((buf,) + args) if alias else args))


def middle_kernel(units, last, sg, act, start_ref, out, total):
    step = pl.program_id(0)
    rows = sg.shape[0]
    pixels = rows * BLK

    @pl.when(step == 0)
    def _():
        total[...] = start_ref[...]

    for u in range(units):
        cols = slice(u * BLK, (u + 1) * BLK)
        turned = jnp.transpose(sg[:, cols, :].reshape(pixels, LANES))
        for a in range(3):
            window = act[a : a + rows, cols, :].reshape(pixels, 3 * LANES)
            total[a] += mm(turned, window)

    @pl.when(step == pl.num_programs(0) - 1)
    def _():
        if last:
            for a in range(3):
                for b in range(3):
                    out[a, b] = jnp.transpose(total[a, :, b * LANES : (b + 1) * LANES])
        else:
            out[...] = total[...]


def middle(sg, act, start, last):
    rows, width, _ = sg.shape
    blocks = width // BLK
    u = unit(blocks, 0, 4)
    shape = (3, 3, LANES, LANES) if last else (3, LANES, 3 * LANES)
    return pl.pallas_call(
        functools.partial(middle_kernel, u, last),
        grid=(blocks // u,),
        in_specs=[
            pl.BlockSpec((rows, u * BLK, LANES), lambda i: (0, i, 0)),
            pl.BlockSpec((rows + 2, u * BLK, 3 * LANES), lambda i: (0, i, 0)),
            whole(start.shape),
        ],
        out_specs=whole(shape),
        out_shape=jax.ShapeDtypeStruct(shape, F32),
        scratch_shapes=[pltpu.VMEM((3, LANES, 3 * LANES), F32)],
        compiler_params=params(),
        cost_estimate=cost(
            2 * rows * width * 9 * LANES * LANES, rows * width * 2 * 4 * LANES
        ),
        name="middle",
    )(sg, act, start)


def close_kernel(units, last, buf_in, sg, taps, fpre, binput, weight, fw_in, buf, fw, total):
    step = pl.program_id(0)
    rows = fpre.shape[0]
    pixels = rows * BLK
    channels = binput.shape[2]

    @pl.when(step == 0)
    def _():
        total[...] = fw_in[...]

    for u in range(units):
        cols = slice(u * BLK, (u + 1) * BLK)
        acc = None
        for a in range(3):
            moved = sg[2 - a : 2 - a + rows, cols, :].reshape(pixels, 3 * LANES)
            part = mm(moved, taps[a])
            acc = part if acc is None else acc + part
        gate = fpre[:, cols, :].reshape(pixels, LANES).astype(F32) > 0
        grad = jnp.where(gate, acc, 0.0).astype(BF)
        total[...] += mm(
            jnp.transpose(grad), binput[:, cols, :].reshape(pixels, channels)
        )
        back = mm_nt(grad, weight[...])
        direct = buf_in[:, cols, :].reshape(pixels, channels).astype(F32)
        buf[:, cols, :] = (back + direct).astype(BF).reshape(rows, BLK, channels)

    @pl.when(step == pl.num_programs(0) - 1)
    def _():
        if last:
            for t in range(channels // LANES):
                fw[t * LANES : (t + 1) * LANES, :] = jnp.transpose(
                    total[:, t * LANES : (t + 1) * LANES]
                )
        else:
            fw[...] = total[...]


def close_block(buf, sg, taps, fpre, binput, weight, fw_in, start, last):
    rows, _, channels = binput.shape
    width = sg.shape[1]
    blocks = width // BLK
    u = unit(blocks, start, 3)
    first = start // u
    wide = lambda c: pl.BlockSpec((rows, u * BLK, c), lambda i: (0, first + i, 0))
    shape = (channels, LANES) if last else (LANES, channels)
    pixels = rows * width
    return pl.pallas_call(
        functools.partial(close_kernel, u, last),
        grid=(blocks // u,),
        in_specs=[
            wide(channels),
            pl.BlockSpec((rows + 2, u * BLK, 3 * LANES), lambda i: (0, i, 0)),
            whole(taps.shape),
            wide(LANES),
            wide(channels),
            whole(weight.shape),
            whole(fw_in.shape),
        ],
        out_specs=[wide(channels), whole(shape)],
        out_shape=[
            jax.ShapeDtypeStruct(buf.shape, BF),
            jax.ShapeDtypeStruct(shape, F32),
        ],
        scratch_shapes=[pltpu.VMEM((LANES, channels), F32)],
        input_output_aliases={0: 0},
        compiler_params=params(),
        cost_estimate=cost(
            2 * pixels * LANES * (9 * LANES + 2 * channels),
            2 * pixels * (3 * channels + 4 * LANES),
        ),
        name="close_block",
    )(buf, sg, taps, fpre, binput, weight, fw_in)


def swap_pairs(value, count):
    return lax.ppermute(value, AXIS, [(i, i ^ 1) for i in range(count)])


def same_core(count):
    return [list(range(c, count, 2)) for c in range(2)]


def scatter_sum(parts, count):
    odd = lax.axis_index(AXIS) % 2 == 1
    pairs = parts.reshape((count // 2, 2) + parts.shape[1:])
    kept = jnp.where(odd, pairs[:, 1], pairs[:, 0])
    given = jnp.where(odd, pairs[:, 0], pairs[:, 1])
    both = kept + swap_pairs(given, count)
    got = lax.all_to_all(
        both, AXIS, 0, 0, tiled=True, axis_index_groups=same_core(count)
    )
    return jnp.sum(got, axis=0)


def gather(share, count):
    odd = lax.axis_index(AXIS) % 2 == 1
    copies = jnp.broadcast_to(share[None], (count // 2,) + share.shape)
    own = lax.all_to_all(
        copies, AXIS, 0, 0, tiled=True, axis_index_groups=same_core(count)
    )
    other = swap_pairs(own, count)
    pairs = jnp.stack([jnp.where(odd, other, own), jnp.where(odd, own, other)], axis=1)
    return pairs.reshape((count * share.shape[0],) + share.shape[1:])


def edges(value, count):
    up = [(i, i + 1) for i in range(count - 1)]
    down = [(i + 1, i) for i in range(count - 1)]
    return lax.ppermute(value[-1:], AXIS, up), lax.ppermute(value[:1], AXIS, down)


def beside(value):
    width = value.shape[1] - 2
    return [value[:, b : b + width] for b in range(3)]


def shards(
    block_input,
    first_pre,
    second_pre,
    output_pre,
    output_grad,
    first_weight,
    middle_weight,
    last_weight,
):
    tile_rows, map_cols, channels = block_input.shape
    inner = first_pre.shape[2]
    count = lax.axis_size(AXIS)
    factor = 1.0 / math.sqrt(tile_rows * map_cols * count)
    own = channels // count
    join = LANES // own
    groups = BLK // join
    blocks = map_cols // BLK
    head = 4 * (3 * blocks // 16)
    tail = blocks - head
    split = head * BLK
    seam = split - BLK

    turned = jnp.transpose(output_grad, (1, 2, 0)).reshape(map_cols * own, -1)
    send_a = pack(turned, count, tile_rows, groups, 0, head)
    recv_a = lax.all_to_all(send_a, AXIS, 0, 0, tiled=True)
    turned, _ = lax.optimization_barrier((turned, send_a))
    send_b = pack(turned, count, tile_rows, groups, head, tail)
    recv_b = lax.all_to_all(send_b, AXIS, 0, 0, tiled=True)

    size = join * LANES
    lane = jnp.arange(size)
    src, col, chan = lane // LANES, lane % LANES // own, lane % own
    lane_sort = (
        (col * LANES + src * own + chan)[:, None] == lane[None, :]
    ).astype(BF)
    pixel = jnp.arange(tile_rows * BLK)
    row, column = pixel // BLK, pixel % BLK
    place = (column % join * groups + column // join) * tile_rows + row
    pixel_sort = (place[:, None] == pixel[None, :]).astype(BF)
    taps = jnp.transpose(middle_weight, (0, 1, 3, 2)).reshape(3, 3 * inner, inner)

    before, after = edges(first_pre, count)
    act = jnp.maximum(jnp.concatenate([before, first_pre, after], axis=0), 0)
    act = jnp.concatenate(beside(jnp.pad(act, ((0, 0), (1, 1), (0, 0)))), axis=2)
    act_a, act_b = act[:, :split], act[:, split:]

    lw0 = jnp.zeros((channels // LANES, inner, LANES), F32)
    buf, sg_a, lw_a = open_block(
        None, recv_a, output_pre, second_pre, lane_sort, pixel_sort, last_weight, lw0, join, 0
    )
    before, after = edges(sg_a, count)
    mw_a = middle(sg_a, act_a, jnp.zeros((3, inner, 3 * inner), F32), False)
    ext_a = jnp.concatenate([before, sg_a, after], axis=0)
    near = jnp.pad(ext_a, ((0, 0), (1, 0), (0, 0)))[:, : seam + 2]
    near = jnp.concatenate(beside(near)[::-1], axis=2)
    buf, fw_a = close_block(
        buf,
        near,
        taps,
        first_pre,
        block_input,
        first_weight,
        jnp.zeros((inner, channels), F32),
        0,
        False,
    )

    buf, sg_b, lw = open_block(
        buf, recv_b, output_pre, second_pre, lane_sort, pixel_sort, last_weight, lw_a, join, head
    )
    before, after = edges(sg_b, count)
    mw = middle(sg_b, act_b, mw_a, True)
    both = jnp.concatenate(
        [mw.reshape(9 * inner, inner), lw.reshape(channels, LANES)], axis=0
    )
    share = scatter_sum(both.reshape(count, -1, LANES), count)
    both = gather(share * factor, count)

    ext_b = jnp.concatenate([before, sg_b, after], axis=0)
    far = jnp.concatenate([ext_a[:, seam - 1 :], ext_b], axis=1)
    far = jnp.pad(far, ((0, 0), (0, 1), (0, 0)))
    far = jnp.concatenate(beside(far)[::-1], axis=2)
    buf, fw = close_block(
        buf, far, taps, first_pre, block_input, first_weight, fw_a, head - 1, True
    )
    first_wgrad = scatter_sum(fw.reshape(count, own, LANES), count) * factor

    middle_wgrad = both[: 9 * inner].reshape(3, 3, inner, inner)
    last_wgrad = (
        both[9 * inner :].reshape(-1, inner, LANES).transpose(1, 0, 2).reshape(inner, channels)
    )
    return (buf, first_wgrad, middle_wgrad, last_wgrad)


def solution(mesh):
    placed = (
        P(("groups", "rows"), None, None),
        P(("groups", "rows"), None, None),
        P(("groups", "rows"), None, None),
        P(("groups", "rows"), None, None),
        P("groups", None, "rows"),
        P(),
        P(),
        P(),
    )
    return jax.shard_map(
        shards,
        mesh=mesh,
        in_specs=placed,
        out_specs=(
            P(("groups", "rows"), None, None),
            P(("groups", "rows"), None),
            P("groups", None, None, None),
            P("groups", None),
        ),
        check_vma=False,
    )
```

time: 378 us -> 230 us (0.61)
  waiting for transfers between devices: 254 us -> 87.9 us
  Pallas kernels: 0 us -> 48.9 us
  starting transfers between devices: 15.5 us -> 61.7 us
  local copies, waits for them, and re-layouts: 48.8 us -> 19.2 us
  matrix products: 25.6 us -> 0 us
  between operations: 14.4 us -> 1.1 us
  other arithmetic: 18 us -> 9.31 us
    psum x1 -> x0, waiting for transfers between devices: 97.3 us -> none  [shards(): middle_total = lax.psum(middle_part, 'rows')]
    unnamed x3 -> x0, waiting for transfers between devices: 55.1 us -> none
    pallas_call x0 -> x8, Pallas kernels: none -> 48.9 us  [the longest x2 19 us: open_block(): return call(*((buf,) + args if alias else args))]
    all_to_all x1 -> x5, starting transfers between devices: 7.56 us -> 49 us  [the longest x1 19.7 us: shards(): recv_b = lax.all_to_all(send_b, AXIS, 0, 0, tiled=True)]
    dot_general x22 -> x0, matrix products: 25.6 us -> none  [the longest x11 12 us: contract_rows(): lax.dot_general(left, right, (((0,), (0,)), ((), ())), preferred_element_...]
    unnamed x43 -> x49, local copies, waits for them, and re-layouts: 27.6 us -> 11.8 us
    all_to_all x1 -> x5, waiting for transfers between devices: 93.3 us -> 82.5 us  [the longest x1 69.4 us: shards(): recv_a = lax.all_to_all(send_a, AXIS, 0, 0, tiled=True)]
    select_n x1 -> x0, local copies, waits for them, and re-layouts: 8.53 us -> none  [shards(): masked_out = jnp.where(output_pre > 0, spatial, jnp.zeros_like(spatial))]
  transfers between devices with their start and end apart: 7 -> 14, of which waited for: 4 -> 7; matrix products, arithmetic and copies ran while one was open for 10% -> 6% of each run, Pallas kernels for 0% -> 16%
where the time goes in v1:
time: 230 us; the launch traced here: 228 us
  waiting for transfers between devices  87.9 us (38%)
  starting transfers between devices  61.7 us (27%)
  Pallas kernels  48.9 us (21%)
  local copies, waits for them, and re-layouts  19.2 us (8%)
  other arithmetic  9.31 us (4%)
    all_to_all x1, waiting for transfers between devices, shards(): recv_a = lax.all_to_all(send_a, AXIS, 0, 0, tiled=True)  69.4 us
    all_to_all x1, starting transfers between devices, shards(): recv_b = lax.all_to_all(send_b, AXIS, 0, 0, tiled=True)  19.7 us
    pallas_call x2, Pallas kernels, open_block(): return call(*((buf,) + args if alias else args))  19 us
    pallas_call x2, Pallas kernels, close_block(): pl.pallas_call(functools.partial(close_kernel, u, last), grid=(blocks //...  18.4 us
    all_to_all x2, starting transfers between devices, scatter_sum(): lax.all_to_all(both, AXIS, 0, 0, tiled=True, axis_index_groups=same_core(...  17.4 us
    all_to_all x2, waiting for transfers between devices, scatter_sum(): lax.all_to_all(both, AXIS, 0, 0, tiled=True, axis_index_groups=same_core(...  12 us
    unnamed x49, local copies, waits for them, and re-layouts  11.8 us
    all_to_all x1, starting transfers between devices, shards(): recv_a = lax.all_to_all(send_a, AXIS, 0, 0, tiled=True)  7.57 us
  transfers between devices with their start and end apart: 14, of which 7 were waited for; matrix products, arithmetic and copies ran while one was open for 6% of the time, Pallas kernels for 16%

profile of v1, /device:TPU:0, one launch (start us, length us, event | category | flops | bytes accessed | tf_op | source)
XLA Modules:
  0.0 228.1 jit_solution(11707161588375977476)
XLA Ops:
  0.7 4.2 %pack.2 = bf16[16,16,64,128]{3,2,1,0:T(8,128)(2,1)S(1)} custom-call(bf16[11264,256]{1,0:T(8,128)(2,1)} %bitcast.63, bf16[256,256]{1,0:T(8,128)(2,1)S(1)} %fusion.3.eye_ref), custom_call_target="tpu_custom_call" | custom-call | flops 1073741824 | bytes 8388608 | tf_op jit(solution)/shard_map/pack/pallas_call | solution.py:76
  4.8 2.0 copy-done
  6.8 7.6 %all-to-all-start = ((bf16[16,16,64,128]{3,2,1,0:T(8,128)(2,1)}), bf16[16,16,64,128]{3,2,1,0:T(8,128)(2,1)}, u32[]{:S(2)}, u32[]{:S(2)}) async-start(bf16[16,16,64,128]{3,2,1,0:T(8,128)(2,1)} %copy-done), calls=%async_computation | async-start | bytes 8388608 | tf_op jit(solution)/shard_map/all_to_all | solution.py:382
  15.1 2.3 collective-permute-start.5
  18.7 2.8 %pack.3 = bf16[16,6,64,128]{3,2,1,0:T(8,128)(2,1)S(1)} custom-call(bf16[11264,256]{1,0:T(8,128)(2,1)} %bitcast.64, bf16[256,256]{1,0:T(8,128)(2,1)S(1)} %fusion.3.eye_ref), custom_call_target="tpu_custom_call" | custom-call | flops 402653184 | bytes 3145728 | tf_op jit(solution)/shard_map/pack/pallas_call | solution.py:76
  22.7 69.4 %all-to-all-done.refs_0_ = bf16[16,16,64,128]{3,2,1,0:T(8,128)(2,1)} async-done(((bf16[16,16,64,128]{3,2,1,0:T(8,128)(2,1)}), bf16[16,16,64,128]{3,2,1,0:T(8,128)(2,1)}, u32[]{:S(2)}, u32[]{:S(2)}) %all-to-all-start) | async-done | bytes 4194336 | tf_op jit(solution)/shard_map/all_to_all | solution.py:382
  92.1 19.7 %all-to-all-start.1 = ((bf16[16,6,64,128]{3,2,1,0:T(8,128)(2,1)}), bf16[16,6,64,128]{3,2,1,0:T(8,128)(2,1)S(1)}, u32[]{:S(2)}, u32[]{:S(2)}) async-start(bf16[16,6,64,128]{3,2,1,0:T(8,128)(2,1)} %copy-done.2), calls=%async_computation.1 | async-start | bytes 3145728 | tf_op jit(solution)/shard_map/all_to_all | solution.py:385
  118.8 12.9 %open_block.2 = (bf16[16,352,512]{2,1,0:T(8,128)(2,1)}, bf16[16,256,128]{2,1,0:T(8,128)(2,1)S(1)}, f32[4,128,128]{2,1,0:T(8,128)S(1)}) custom-call(bf16[16,16,64,128]{3,2,1,0:T(8,128)(2,1)} %all-to-all-done.refs_0_, bf16[16,352,512]{2,1,0:T(8,128)(2,1)} %refs_2_.3, bf16[16,352,128]{2,1,0:T(8,128)(2,1)S(1)} %copy-done.10, bf16[512,512]{1,0:T(8,128)(2,1)S(1)} %copy-done.6, ...), custom_call_target="tpu_custom_call" | custom-call | flops 4294967296 | bytes 14680064 | tf_op jit(solution)/shard_map/open_block/pallas_call | solution.py:188
  133.0 3.0 %collective-permute-start = (bf16[1,256,128]{2,1,0:T(8,128)(2,1)S(1)}, bf16[1,256,128]{2,1,0:T(8,128)(2,1)S(1)}, u32[]{:S(2)}, u32[]{:S(2)}) collective-permute-start(bf16[1,256,128]{2,1,0:T(8,128)(2,1)S(1)} %get-tuple-element.38), channel_id=1, source_target_pairs={{0,1},{1,2},{2,3},{3,4},{4,5},{5,6},{6,7},{7,8},{8,9},{9,10},{10,1... | collective-permute-start | bytes 196616 | tf_op jit(solution)/shard_map/ppermute | solution.py:349
  136.1 3.1 %middle.2.start_ref = f32[3,128,384]{2,1,0:T(8,128)S(1)} custom-call(bf16[16,256,128]{2,1,0:T(8,128)(2,1)S(1)} %get-tuple-element.16.sg, bf16[18,256,384]{2,1,0:T(8,128)(2,1)S(1)} %pad_maximum_fusion.act, f32[3,128,384]{2,1,0:T(8,128)S(1)} %broadcast_in_dim.10.start_ref), custom_call_target="tpu_custom_call" | custom-call | flops 1207959552 | bytes 4194304 | tf_op jit(solution)/shard_map/middle/pallas_call | solution.py:222
  141.4 10.4 %close_block.2 = (bf16[16,352,512]{2,1,0:T(8,128)(2,1)}, f32[128,512]{1,0:T(8,128)S(1)}) custom-call(bf16[16,352,512]{2,1,0:T(8,128)(2,1)} %get-tuple-element.15.buf_in, bf16[18,240,384]{2,1,0:T(8,128)(2,1)S(1)} %pad_maximum_fusion.2.sg, bf16[3,384,128]{2,1,0:T(8,128)(2,1)S(1)} %bitcast.57, ...), custom_call_target="tpu_custom_call", output_to_operand_aliasing={{0}: (0, {})} | custom-call | flops 2139095040 | bytes 15728640 | tf_op jit(solution)/shard_map/close_block/pallas_call | solution.py:287
  153.6 1.4 copy-done.11
  157.7 6.1 %open_block.3 = (bf16[16,352,512]{2,1,0:T(8,128)(2,1)}, bf16[16,96,128]{2,1,0:T(8,128)(2,1)S(1)}, f32[4,128,128]{2,1,0:T(8,128)S(1)}) custom-call(bf16[16,352,512]{2,1,0:T(8,128)(2,1)} %get-tuple-element.17.refs_0_, bf16[16,6,64,128]{3,2,1,0:T(8,128)(2,1)S(1)} %all-to-all-done.1.refs_1_, ...), custom_call_target="tpu_custom_call", output_to_operand_aliasing={{0}: (0, {})} | custom-call | flops 1610612736 | bytes 5505024 | tf_op jit(solution)/shard_map/open_block/pallas_call | solution.py:188
  163.8 1.5 middle.3
  165.4 1.7 collective-permute-start.7
  167.2 1.4 collective-permute-done.7
  169.4 12.5 %all-to-all-start.3 = ((f32[8,104,128]{2,1,0:T(8,128)}), f32[8,104,128]{2,1,0:T(8,128)S(1)}, u32[]{:S(2)}, u32[]{:S(2)}) async-start(f32[8,104,128]{2,1,0:T(8,128)} %fusion.2), calls=%async_computation.3 | async-start | bytes 851968 | tf_op jit(solution)/shard_map/all_to_all | solution.py:329
  181.9 1.8 collective-permute-start.2
  185.9 2.6 %collective-permute-done.3 = bf16[1,96,128]{2,1,0:T(8,128)(2,1)S(1)} collective-permute-done((bf16[1,96,128]{2,1,0:T(8,128)(2,1)S(1)}, bf16[1,96,128]{2,1,0:T(8,128)(2,1)S(1)}, u32[]{:S(2)}, u32[]{:S(2)}) %collective-permute-start.3) | collective-permute-done | bytes 24608 | tf_op jit(solution)/shard_map/ppermute | solution.py:349
  189.9 4.7 %all-to-all-done.3 = f32[8,104,128]{2,1,0:T(8,128)S(1)} async-done(((f32[8,104,128]{2,1,0:T(8,128)}), f32[8,104,128]{2,1,0:T(8,128)S(1)}, u32[]{:S(2)}, u32[]{:S(2)}) %all-to-all-start.3) | async-done | bytes 426016 | tf_op jit(solution)/shard_map/all_to_all | solution.py:329
  195.4 4.3 %all-to-all-start.4 = ((f32[8,104,128]{2,1,0:T(8,128)}), f32[8,104,128]{2,1,0:T(8,128)}, u32[]{:S(2)}, u32[]{:S(2)}) async-start(f32[8,104,128]{2,1,0:T(8,128)} %broadcast_in_dim.22), calls=%async_computation.4 | async-start | bytes 851968 | tf_op jit(solution)/shard_map/all_to_all | solution.py:338
  201.1 7.9 %close_block.3 = (bf16[16,352,512]{2,1,0:T(8,128)(2,1)}, f32[512,128]{1,0:T(8,128)S(1)}) custom-call(bf16[16,352,512]{2,1,0:T(8,128)(2,1)} %get-tuple-element.20.buf_in, bf16[18,112,384]{2,1,0:T(8,128)(2,1)S(1)} %pad_maximum_fusion.3.sg, bf16[3,384,128]{2,1,0:T(8,128)(2,1)S(1)} %bitcast.58, ...), custom_call_target="tpu_custom_call", output_to_operand_aliasing={{0}: (0, {})} | custom-call | flops 998244352 | bytes 7340032 | tf_op jit(solution)/shard_map/close_block/pallas_call | solution.py:287
  212.2 4.9 %all-to-all-start.2 = ((f32[8,32,128]{2,1,0:T(8,128)}), f32[8,32,128]{2,1,0:T(8,128)S(1)}, u32[]{:S(2)}, u32[]{:S(2)}) async-start(f32[8,32,128]{2,1,0:T(8,128)} %fusion.6), calls=%async_computation.2 | async-start | bytes 262144 | tf_op jit(solution)/shard_map/all_to_all | solution.py:329
  217.1 7.3 %all-to-all-done.2 = f32[8,32,128]{2,1,0:T(8,128)S(1)} async-done(((f32[8,32,128]{2,1,0:T(8,128)}), f32[8,32,128]{2,1,0:T(8,128)S(1)}, u32[]{:S(2)}, u32[]{:S(2)}) %all-to-all-start.2) | async-done | bytes 131104 | tf_op jit(solution)/shard_map/all_to_all | solution.py:329
  (99 shorter events, 31.5 us)
Async XLA Ops:
  4.8 2.0 copy-start
  6.8 7.6 %copy-start.1 = (bf16[16,352,128]{2,1,0:T(8,128)(2,1)S(1)}, bf16[16,352,128]{2,1,0:T(8,128)(2,1)}, u32[]{:S(2)}) copy-start(bf16[16,352,128]{2,1,0:T(8,128)(2,1)} %fpre.3) | copy-start | bytes 4325380
  6.8 85.3 %all-to-all-start = ((bf16[16,16,64,128]{3,2,1,0:T(8,128)(2,1)}), bf16[16,16,64,128]{3,2,1,0:T(8,128)(2,1)}, u32[]{:S(2)}, u32[]{:S(2)}) async-start(bf16[16,16,64,128]{3,2,1,0:T(8,128)(2,1)} %copy-done), calls=%async_computation | async-start | bytes 8388608 | tf_op jit(solution)/shard_map/all_to_all | solution.py:382
  15.1 99.0 %collective-permute-start.5 = (bf16[1,352,128]{2,1,0:T(8,128)(2,1)}, bf16[1,352,128]{2,1,0:T(8,128)(2,1)S(1)}, u32[]{:S(2)}, u32[]{:S(2)}) collective-permute-start(bf16[1,352,128]{2,1,0:T(8,128)(2,1)} %get-tuple-element.32), channel_id=1, source_target_pairs={{0,1},{1,2},{2,3},{3,4},{4,5},{5,6},{6,7},{7,8},{8,9},{9,10},{10,1... | collective-permute-start | bytes 270344 | tf_op jit(solution)/shard_map/ppermute | solution.py:349
  17.4 96.8 %collective-permute-start.6 = (bf16[1,352,128]{2,1,0:T(8,128)(2,1)}, bf16[1,352,128]{2,1,0:T(8,128)(2,1)}, u32[]{:S(2)}, u32[]{:S(2)}) collective-permute-start(bf16[1,352,128]{2,1,0:T(8,128)(2,1)} %get-tuple-element.33), channel_id=1, source_target_pairs={{1,0},{2,1},{3,2},{4,3},{5,4},{6,5},{7,6},{8,7},{9,8},{10,9},{11,1... | collective-permute-start | bytes 270344 | tf_op jit(solution)/shard_map/ppermute | solution.py:349
  92.1 60.4 %all-to-all-start.1 = ((bf16[16,6,64,128]{3,2,1,0:T(8,128)(2,1)}), bf16[16,6,64,128]{3,2,1,0:T(8,128)(2,1)S(1)}, u32[]{:S(2)}, u32[]{:S(2)}) async-start(bf16[16,6,64,128]{3,2,1,0:T(8,128)(2,1)} %copy-done.2), calls=%async_computation.1 | async-start | bytes 3145728 | tf_op jit(solution)/shard_map/all_to_all | solution.py:385
  112.9 4.9 %copy-start.13 = (bf16[256,256]{1,0:T(8,128)(2,1)}, bf16[256,256]{1,0:T(8,128)(2,1)S(1)}, u32[]{:S(2)}) copy-start(bf16[256,256]{1,0:T(8,128)(2,1)S(1)} %fusion.4.refs_4_.refs_5_) | copy-start | bytes 393220
  117.3 1.5 copy-start.19
  131.7 4.4 %copy-start.17 = (f32[4,128,128]{2,1,0:T(8,128)}, f32[4,128,128]{2,1,0:T(8,128)S(1)}, u32[]{:S(2)}) copy-start(f32[4,128,128]{2,1,0:T(8,128)S(1)} %get-tuple-element.19.refs_7_) | copy-start | bytes 786436
  131.7 7.7 %collective-permute-start.1 = (bf16[1,256,128]{2,1,0:T(8,128)(2,1)S(1)}, bf16[1,256,128]{2,1,0:T(8,128)(2,1)S(1)}, u32[]{:S(2)}, u32[]{:S(2)}) collective-permute-start(bf16[1,256,128]{2,1,0:T(8,128)(2,1)S(1)} %get-tuple-element.37), channel_id=1, source_target_pairs={{1,0},{2,1},{3,2},{4,3},{5,4},{6,5},{7,6},{8,7},{9,8},{10,9},{11,1... | collective-permute-start | bytes 196616 | tf_op jit(solution)/shard_map/ppermute | solution.py:349
  133.0 6.2 %collective-permute-start = (bf16[1,256,128]{2,1,0:T(8,128)(2,1)S(1)}, bf16[1,256,128]{2,1,0:T(8,128)(2,1)S(1)}, u32[]{:S(2)}, u32[]{:S(2)}) collective-permute-start(bf16[1,256,128]{2,1,0:T(8,128)(2,1)S(1)} %get-tuple-element.38), channel_id=1, source_target_pairs={{0,1},{1,2},{2,3},{3,4},{4,5},{5,6},{6,7},{7,8},{8,9},{9,10},{10,1... | collective-permute-start | bytes 196616 | tf_op jit(solution)/shard_map/ppermute | solution.py:349
  157.7 6.1 %copy-start.3 = (bf16[18,96,384]{2,1,0:T(8,128)(2,1)S(1)}, bf16[18,96,384]{2,1,0:T(8,128)(2,1)}, u32[]{:S(2)}) copy-start(bf16[18,96,384]{2,1,0:T(8,128)(2,1)} %pad_maximum_fusion.4.act) | copy-start | bytes 3981316
  157.7 6.1 %copy-start.5 = (f32[3,128,384]{2,1,0:T(8,128)S(1)}, f32[3,128,384]{2,1,0:T(8,128)}, u32[]{:S(2)}) copy-start(f32[3,128,384]{2,1,0:T(8,128)} %copy-done.4) | copy-start | bytes 1769476
  163.8 1.6 copy-start.8
  165.4 16.5 %copy-start.9 = (bf16[16,96,128]{2,1,0:T(8,128)(2,1)S(1)}, bf16[16,96,128]{2,1,0:T(8,128)(2,1)}, u32[]{:S(2)}) copy-start(bf16[16,96,128]{2,1,0:T(8,128)(2,1)} %copy-done.8) | copy-start | bytes 1179652
  165.4 3.1 %collective-permute-start.7 = (f32[8,104,128]{2,1,0:T(8,128)S(1)}, f32[8,104,128]{2,1,0:T(8,128)S(1)}, u32[]{:S(2)}, u32[]{:S(2)}) collective-permute-start(f32[8,104,128]{2,1,0:T(8,128)S(1)} %select_bitcast_fusion.2), channel_id=1, source_target_pairs={{0,1},{1,0},{2,3},{3,2},{4,5},{5,4},{6,7},{7,6},{8,9},{9,8},{10,11... | collective-permute-start | bytes 1277960 | tf_op jit(solution)/shard_map/ppermute | solution.py:316
  169.4 25.2 %all-to-all-start.3 = ((f32[8,104,128]{2,1,0:T(8,128)}), f32[8,104,128]{2,1,0:T(8,128)S(1)}, u32[]{:S(2)}, u32[]{:S(2)}) async-start(f32[8,104,128]{2,1,0:T(8,128)} %fusion.2), calls=%async_computation.3 | async-start | bytes 851968 | tf_op jit(solution)/shard_map/all_to_all | solution.py:329
  181.9 4.0 %collective-permute-start.2 = (bf16[1,96,128]{2,1,0:T(8,128)(2,1)S(1)}, bf16[1,96,128]{2,1,0:T(8,128)(2,1)S(1)}, u32[]{:S(2)}, u32[]{:S(2)}) collective-permute-start(bf16[1,96,128]{2,1,0:T(8,128)(2,1)S(1)} %get-tuple-element.44), channel_id=1, source_target_pairs={{0,1},{1,2},{2,3},{3,4},{4,5},{5,6},{6,7},{7,8},{8,9},{9,10},{10,1... | collective-permute-start | bytes 73736 | tf_op jit(solution)/shard_map/ppermute | solution.py:349
  183.7 4.9 %collective-permute-start.3 = (bf16[1,96,128]{2,1,0:T(8,128)(2,1)S(1)}, bf16[1,96,128]{2,1,0:T(8,128)(2,1)S(1)}, u32[]{:S(2)}, u32[]{:S(2)}) collective-permute-start(bf16[1,96,128]{2,1,0:T(8,128)(2,1)S(1)} %get-tuple-element.45), channel_id=1, source_target_pairs={{1,0},{2,1},{3,2},{4,3},{5,4},{6,5},{7,6},{8,7},{9,8},{10,9},{11,1... | collective-permute-start | bytes 73736 | tf_op jit(solution)/shard_map/ppermute | solution.py:349
  189.9 9.9 %copy-start.22 = (bf16[18,112,128]{2,1,0:T(8,128)(2,1)S(1)}, bf16[18,112,128]{2,1,0:T(8,128)(2,1)}, u32[]{:S(2)}) copy-start(bf16[18,112,128]{2,1,0:T(8,128)(2,1)} %get-tuple-element.42) | copy-start | bytes 1548292
  195.4 16.8 %all-to-all-start.4 = ((f32[8,104,128]{2,1,0:T(8,128)}), f32[8,104,128]{2,1,0:T(8,128)}, u32[]{:S(2)}, u32[]{:S(2)}) async-start(f32[8,104,128]{2,1,0:T(8,128)} %broadcast_in_dim.22), calls=%async_computation.4 | async-start | bytes 851968 | tf_op jit(solution)/shard_map/all_to_all | solution.py:338
  209.0 1.4 collective-permute-start.4
  212.2 12.2 %all-to-all-start.2 = ((f32[8,32,128]{2,1,0:T(8,128)}), f32[8,32,128]{2,1,0:T(8,128)S(1)}, u32[]{:S(2)}, u32[]{:S(2)}) async-start(f32[8,32,128]{2,1,0:T(8,128)} %fusion.6), calls=%async_computation.2 | async-start | bytes 262144 | tf_op jit(solution)/shard_map/all_to_all | solution.py:329
  217.1 8.0 %collective-permute-start.8 = (f32[8,104,128]{2,1,0:T(8,128)}, f32[8,104,128]{2,1,0:T(8,128)S(1)}, u32[]{:S(2)}, u32[]{:S(2)}) collective-permute-start(f32[8,104,128]{2,1,0:T(8,128)} %all-to-all-done.4), channel_id=1, source_target_pairs={{0,1},{1,0},{2,3},{3,2},{4,5},{5,4},{6,7},{7,6},{8,9},{9,8},{10,11... | collective-permute-start | bytes 1277960 | tf_op jit(solution)/shard_map/ppermute | solution.py:316
  (13 other events, 13.8 us)

commit v2 on v1

v2 whole, which is shorter than its diff:
```python
import functools
import math

import jax
import jax.numpy as jnp
from jax import lax
from jax.experimental import pallas as pl
from jax.experimental.pallas import tpu as pltpu
from jax.sharding import PartitionSpec as P

BF = jnp.bfloat16
F32 = jnp.float32
AXIS = "rows"
BLK = 16
LANES = 128


def dims(lhs, rhs):
    return (((lhs,), (rhs,)), ((), ()))


def mm(a, b):
    return lax.dot_general(a, b, dims(1, 0), preferred_element_type=F32)


def mm_nt(a, b):
    return lax.dot_general(a, b, dims(1, 1), preferred_element_type=F32)


def unit(count, offset, cap):
    return max(u for u in range(1, cap + 1) if count % u == 0 and offset % u == 0)


def params():
    return pltpu.CompilerParams(
        dimension_semantics=("arbitrary",), vmem_limit_bytes=24 * 2**20
    )


def hbm(value):
    return pltpu.with_memory_space_constraint(value, pltpu.HBM)


def cost(flops, nbytes):
    return pl.CostEstimate(
        flops=int(flops) // 64, transcendentals=0, bytes_accessed=int(nbytes) // 64
    )


def whole(shape):
    zeros = (0,) * len(shape)
    return pl.BlockSpec(shape, lambda i: zeros)


def eye(size):
    a = lax.broadcasted_iota(jnp.int32, (size, size), 0)
    b = lax.broadcasted_iota(jnp.int32, (size, size), 1)
    return (a == b).astype(BF)


def pack_kernel(tile_rows, units, groups, x_ref, eye_ref, out_ref):
    side = eye_ref.shape[0]
    per = side // tile_rows
    depth = groups * LANES
    for u in range(units):
        for h in range(x_ref.shape[1] // side):
            part = x_ref[u * depth : (u + 1) * depth, h * side : (h + 1) * side]
            turned = mm_nt(eye_ref[...], part).astype(BF)
            for g in range(groups):
                piece = turned[:, g * LANES : (g + 1) * LANES]
                out_ref[
                    h * per : (h + 1) * per, u, g * tile_rows : (g + 1) * tile_rows, :
                ] = piece.reshape(per, tile_rows, LANES)


def pack(x, count, tile_rows, groups, start, blocks):
    depth = groups * LANES
    height = x.shape[1]
    side = 256 if height % 256 == 0 else LANES
    u = unit(blocks, start, 4)
    first = start // u
    return pl.pallas_call(
        functools.partial(pack_kernel, tile_rows, u, groups),
        grid=(blocks // u,),
        in_specs=[
            pl.BlockSpec((u * depth, height), lambda i: (first + i, 0)),
            whole((side, side)),
        ],
        out_specs=pl.BlockSpec(
            (count, u, groups * tile_rows, LANES), lambda i: (0, i, 0, 0)
        ),
        out_shape=pltpu.HBM((count, blocks, groups * tile_rows, LANES), BF),
        compiler_params=params(),
        cost_estimate=cost(
            2 * height * side * blocks * depth, 4 * blocks * depth * height
        ),
        name="pack",
    )(hbm(x), eye(side))


def open_kernel(units, join, alias, *refs):
    if alias:
        refs = refs[1:]
    (recv, opre, spre, lanes_ref, pixels_ref, weight, lw_in, buf, sg, lw) = refs
    rows = opre.shape[0]
    tiles = recv.shape[0] // join
    height = recv.shape[2]
    pixels = rows * units * BLK

    @pl.when(pl.program_id(0) == 0)
    def _():
        lw[...] = lw_in[...]

    stack = jnp.concatenate(
        [
            jnp.concatenate([recv[t * join + s, u] for s in range(join)], axis=1)
            for u in range(units)
            for t in range(tiles)
        ],
        axis=0,
    )
    sorted_lanes = mm(stack, lanes_ref[...]).astype(BF)
    spatial = []
    for u in range(units):
        by_pixel = jnp.concatenate(
            [
                jnp.concatenate(
                    [
                        sorted_lanes[
                            (u * tiles + t) * height : (u * tiles + t + 1) * height,
                            j * LANES : (j + 1) * LANES,
                        ]
                        for t in range(tiles)
                    ],
                    axis=1,
                )
                for j in range(join)
            ],
            axis=0,
        )
        spatial.append(
            mm(pixels_ref[...], by_pixel).reshape(rows, BLK, tiles * LANES)
        )
    spatial = jnp.concatenate(spatial, axis=1).reshape(pixels, tiles * LANES)
    gate = opre[...].reshape(pixels, tiles * LANES).astype(F32) > 0
    masked = jnp.where(gate, spatial, 0.0).astype(BF)
    buf[...] = masked.reshape(buf.shape)
    pre = spre[...].reshape(pixels, LANES).astype(F32)
    inner = mm_nt(masked, weight[...])
    sg[...] = jnp.where(pre > 0, inner, 0.0).astype(BF).reshape(sg.shape)
    act = jnp.maximum(pre, 0.0).astype(BF)
    part = mm(jnp.transpose(act), masked)
    for t in range(tiles):
        lw[t] += part[:, t * LANES : (t + 1) * LANES]


def open_block(buf, recv, opre, spre, lane_sort, pixel_sort, weight, lw_in, join, start):
    rows, _, channels = opre.shape
    count, blocks, height, _ = recv.shape
    tiles = channels // LANES
    u = unit(blocks, start, 4)
    first = start // u
    alias = buf is not None
    wide = lambda c: pl.BlockSpec((rows, u * BLK, c), lambda i: (0, first + i, 0))
    pixels = rows * BLK * blocks
    call = pl.pallas_call(
        functools.partial(open_kernel, u, join, alias),
        grid=(blocks // u,),
        in_specs=([pl.BlockSpec(memory_space=pl.ANY)] if alias else [])
        + [
            pl.BlockSpec((count, u, height, LANES), lambda i: (0, i, 0, 0)),
            wide(channels),
            wide(LANES),
            whole(lane_sort.shape),
            whole(pixel_sort.shape),
            whole(weight.shape),
            whole(lw_in.shape),
        ],
        out_specs=[
            wide(channels),
            pl.BlockSpec((rows, u * BLK, LANES), lambda i: (0, i, 0)),
            whole(lw_in.shape),
        ],
        out_shape=[
            jax.ShapeDtypeStruct(opre.shape, BF),
            jax.ShapeDtypeStruct((rows, blocks * BLK, LANES), BF),
            jax.ShapeDtypeStruct(lw_in.shape, F32),
        ],
        input_output_aliases={0: 0} if alias else {},
        compiler_params=params(),
        cost_estimate=cost(
            2 * pixels * channels * (512 + 256 + 256), 2 * pixels * (3 * channels + 256)
        ),
        name="open_block",
    )
    args = (hbm(recv), hbm(opre), hbm(spre), lane_sort, pixel_sort, weight, lw_in)
    return call(*(((buf,) + args) if alias else args))


def middle_kernel(units, sg, act, start_ref, *refs):
    lw, rim, rim_act, out, total = refs if len(refs) == 5 else (None,) * 3 + refs
    step = pl.program_id(0)
    rows = sg.shape[0]
    pixels = rows * units * BLK

    @pl.when(step == 0)
    def _():
        total[...] = start_ref[...]

    turned = jnp.transpose(sg[...].reshape(pixels, LANES))
    for a in range(3):
        window = act[a : a + rows].reshape(pixels, 3 * LANES)
        total[a] += mm(turned, window)

    @pl.when(step == pl.num_programs(0) - 1)
    def _():
        if lw is None:
            out[...] = total[...]
        else:
            for e in range(2):
                total[2 - 2 * e] += mm(jnp.transpose(rim[e]), rim_act[e])
            for a in range(3):
                for b in range(3):
                    top = (3 * a + b) * LANES
                    out[top : top + LANES, :] = jnp.transpose(
                        total[a, :, b * LANES : (b + 1) * LANES]
                    )
            for t in range(lw.shape[0]):
                top = (9 + t) * LANES
                out[top : top + LANES, :] = lw[t]


def middle(sg, act, start, lw=None, rim=None, rim_act=None):
    rows, width, _ = sg.shape
    blocks = width // BLK
    u = unit(blocks, 0, 4)
    extra = () if lw is None else (lw, rim, rim_act)
    shape = start.shape if lw is None else ((9 + lw.shape[0]) * LANES, LANES)
    return pl.pallas_call(
        functools.partial(middle_kernel, u),
        grid=(blocks // u,),
        in_specs=[
            pl.BlockSpec((rows, u * BLK, LANES), lambda i: (0, i, 0)),
            pl.BlockSpec((rows + 2, u * BLK, 3 * LANES), lambda i: (0, i, 0)),
            whole(start.shape),
        ]
        + [whole(e.shape) for e in extra],
        out_specs=whole(shape),
        out_shape=jax.ShapeDtypeStruct(shape, F32),
        scratch_shapes=[pltpu.VMEM((3, LANES, 3 * LANES), F32)],
        compiler_params=params(),
        cost_estimate=cost(
            2 * rows * width * 9 * LANES * LANES, rows * width * 2 * 4 * LANES
        ),
        name="middle",
    )(sg, act, start, *extra)


def add_pixels(moved, taps, fpre, binput, weight, direct, total):
    acc = None
    for a in range(3):
        part = mm(moved[2 - a], taps[a])
        acc = part if acc is None else acc + part
    grad = jnp.where(fpre.astype(F32) > 0, acc, 0.0).astype(BF)
    total[...] += mm(jnp.transpose(grad), binput)
    return (mm_nt(grad, weight) + direct.astype(F32)).astype(BF)


def close_kernel(units, buf_in, sg, taps, fpre, binput, weight, fw_in, buf, fw):
    rows = fpre.shape[0] - 2
    pixels = rows * units * BLK
    channels = binput.shape[2]

    @pl.when(pl.program_id(0) == 0)
    def _():
        fw[...] = fw_in[...]

    inside = slice(1, 1 + rows)
    out = add_pixels(
        [sg[e : e + rows].reshape(pixels, 3 * LANES) for e in range(3)],
        taps,
        fpre[inside].reshape(pixels, LANES),
        binput[inside].reshape(pixels, channels),
        weight[...],
        buf_in[inside].reshape(pixels, channels),
        fw,
    )
    buf[inside] = out.reshape(rows, units * BLK, channels)
    for e in (0, rows + 1):
        buf[e] = buf_in[e]


def close_block(buf, sg, taps, fpre, binput, weight, fw_in, start):
    rows, _, channels = binput.shape
    width = sg.shape[1]
    blocks = width // BLK
    u = unit(blocks, start, 3)
    first = start // u
    wide = lambda c: pl.BlockSpec((rows, u * BLK, c), lambda i: (0, first + i, 0))
    pixels = rows * width
    return pl.pallas_call(
        functools.partial(close_kernel, u),
        grid=(blocks // u,),
        in_specs=[
            wide(channels),
            pl.BlockSpec((sg.shape[0], u * BLK, 3 * LANES), lambda i: (0, i, 0)),
            whole(taps.shape),
            wide(LANES),
            wide(channels),
            whole(weight.shape),
            whole(fw_in.shape),
        ],
        out_specs=[wide(channels), whole(fw_in.shape)],
        out_shape=[
            jax.ShapeDtypeStruct(buf.shape, BF),
            jax.ShapeDtypeStruct(fw_in.shape, F32),
        ],
        input_output_aliases={0: 0},
        compiler_params=params(),
        cost_estimate=cost(
            2 * pixels * LANES * (9 * LANES + 2 * channels),
            2 * pixels * (3 * channels + 4 * LANES),
        ),
        name="close_block",
    )(buf, sg, taps, hbm(fpre), hbm(binput), weight, fw_in)


def edge_kernel(buf_in, sg, taps, fpre, binput, weight, fw_in, buf, fw, total):
    step = pl.program_id(0)

    @pl.when(step == 0)
    def _():
        total[...] = fw_in[...]

    buf[0] = add_pixels(
        [sg[0, e] for e in range(3)],
        taps,
        fpre[0],
        binput[0],
        weight[...],
        buf_in[0],
        total,
    )

    @pl.when(step == pl.num_programs(0) - 1)
    def _():
        for t in range(binput.shape[2] // LANES):
            fw[t * LANES : (t + 1) * LANES, :] = jnp.transpose(
                total[:, t * LANES : (t + 1) * LANES]
            )


def close_edges(buf, sg, taps, fpre, binput, weight, fw_in):
    rows, _, channels = binput.shape
    width = sg.shape[2]
    flat = lambda c: pl.BlockSpec((1, width, c), lambda i: (i * (rows - 1), 0, 0))
    return pl.pallas_call(
        edge_kernel,
        grid=(2,),
        in_specs=[
            flat(channels),
            pl.BlockSpec((1, 3, width, 3 * LANES), lambda i: (i, 0, 0, 0)),
            whole(taps.shape),
            flat(LANES),
            flat(channels),
            whole(weight.shape),
            whole(fw_in.shape),
        ],
        out_specs=[flat(channels), whole((channels, LANES))],
        out_shape=[
            jax.ShapeDtypeStruct(buf.shape, BF),
            jax.ShapeDtypeStruct((channels, LANES), F32),
        ],
        scratch_shapes=[pltpu.VMEM(fw_in.shape, F32)],
        input_output_aliases={0: 0},
        compiler_params=params(),
        cost_estimate=cost(
            4 * width * LANES * (9 * LANES + 2 * channels), 12 * width * channels
        ),
        name="close_edges",
    )(buf, sg, taps, hbm(fpre), hbm(binput), weight, fw_in)


def exchange(value):
    return lax.all_to_all(value, AXIS, 0, 0, tiled=True)


def exchange_chips(value, count):
    same_core = [list(range(c, count, 2)) for c in range(2)]
    return lax.all_to_all(value, AXIS, 0, 0, tiled=True, axis_index_groups=same_core)


def swap_cores(value, count):
    return lax.ppermute(value, AXIS, [(i, i ^ 1) for i in range(count)])


def edges(value, count):
    up = [(i, i + 1) for i in range(count - 1)]
    down = [(i + 1, i) for i in range(count - 1)]
    return lax.ppermute(value[-1:], AXIS, up), lax.ppermute(value[:1], AXIS, down)


def sorted_taps(ext, width):
    return jnp.concatenate(beside(ext[:, : width + 2])[::-1], axis=2)


def beside(value):
    width = value.shape[1] - 2
    return [value[:, b : b + width] for b in range(3)]


def shards(
    block_input,
    first_pre,
    second_pre,
    output_pre,
    output_grad,
    first_weight,
    middle_weight,
    last_weight,
):
    tile_rows, map_cols, channels = block_input.shape
    inner = first_pre.shape[2]
    count = lax.axis_size(AXIS)
    factor = 1.0 / math.sqrt(tile_rows * map_cols * count)
    own = channels // count
    join = LANES // own
    groups = BLK // join
    blocks = map_cols // BLK
    head = 4 * (3 * blocks // 16)
    tail = blocks - head
    split = head * BLK
    closed = head - 2
    seam = closed * BLK

    turned = jnp.transpose(output_grad, (1, 2, 0)).reshape(map_cols * own, -1)
    send_a = pack(turned, count, tile_rows, groups, 0, head)
    recv_a = exchange(send_a)
    turned, first_pre, _ = lax.optimization_barrier((turned, first_pre, send_a))
    send_b = pack(turned, count, tile_rows, groups, head, tail)

    size = join * LANES
    lane = jnp.arange(size)
    src, col, chan = lane // LANES, lane % LANES // own, lane % own
    lane_sort = (
        (col * LANES + src * own + chan)[:, None] == lane[None, :]
    ).astype(BF)
    pixel = jnp.arange(tile_rows * BLK)
    row, column = pixel // BLK, pixel % BLK
    place = (column % join * groups + column // join) * tile_rows + row
    pixel_sort = (place[:, None] == pixel[None, :]).astype(BF)
    taps = jnp.transpose(middle_weight, (0, 1, 3, 2)).reshape(3, 3 * inner, inner)

    act = jnp.pad(jnp.maximum(first_pre, 0), ((1, 1), (1, 1), (0, 0)))
    act = jnp.concatenate(beside(act), axis=2)
    act_a, act_b = act[:, :split], act[:, split:]
    rim_act = jnp.concatenate([act[1:2], act[-2:-1]], axis=0)
    lw0 = jnp.zeros((channels // LANES, inner, LANES), F32)
    mw0 = jnp.zeros((3, inner, 3 * inner), F32)
    fw0 = jnp.zeros((inner, channels), F32)

    (send_b, lane_sort, pixel_sort, taps, act_a, act_b, rim_act, lw0, mw0, fw0) = (
        lax.optimization_barrier(
            (send_b, lane_sort, pixel_sort, taps, act_a, act_b, rim_act, lw0, mw0, fw0)
        )
    )
    recv_b = exchange(send_b)
    sorts = (lane_sort, pixel_sort)

    buf, sg_a, lw = open_block(
        None, recv_a, output_pre, second_pre, *sorts, last_weight, lw0, join, 0
    )
    mw = middle(sg_a, act_a, mw0)
    left = jnp.pad(sg_a, ((0, 0), (1, 0), (0, 0)))
    buf, fw = close_block(
        buf,
        sorted_taps(left, seam),
        taps,
        first_pre,
        block_input,
        first_weight,
        fw0,
        0,
    )

    lw, mw, fw = lax.optimization_barrier((lw, mw, fw))
    buf, sg_b, lw = open_block(
        buf, recv_b, output_pre, second_pre, *sorts, last_weight, lw, join, head
    )
    rims = jnp.concatenate(
        [
            jnp.concatenate([sg_a[e : e + 1], sg_b[e : e + 1]], axis=1)
            for e in (0, tile_rows - 1)
        ],
        axis=0,
    )
    before, after = edges(rims, count)
    both = middle(
        sg_b, act_b, mw, lw, jnp.concatenate([before, after], axis=0), rim_act
    )

    odd = lax.axis_index(AXIS) % 2 == 1
    half = both.shape[0] // 2
    size = half // (count // 2)
    pair = (both[:half], both[half:])
    kept, given = jnp.where(odd, pair[1], pair[0]), jnp.where(odd, pair[0], pair[1])
    part = (kept + swap_cores(given, count)).astype(BF).reshape(-1, size, LANES)
    part, fw, sg_b = lax.optimization_barrier((part, fw, sg_b))
    parts = exchange_chips(part, count).astype(F32)
    share = (jnp.sum(parts, axis=0) * factor).astype(BF)

    far = jnp.concatenate([sg_a[:, seam - 1 :], sg_b], axis=1)
    far = jnp.pad(far, ((0, 0), (0, 1), (0, 0)))
    buf, fw = close_block(
        buf,
        sorted_taps(far, map_cols - seam),
        taps,
        first_pre,
        block_input,
        first_weight,
        fw,
        closed,
    )
    low = jnp.concatenate([sg_a[:2], sg_b[:2]], axis=1)
    high = jnp.concatenate([sg_a[-2:], sg_b[-2:]], axis=1)
    rim = jnp.concatenate([before, low, high, after], axis=0)
    rim = sorted_taps(jnp.pad(rim, ((0, 0), (1, 1), (0, 0))), map_cols)
    buf, fw = close_edges(
        buf,
        rim.reshape(2, 3, map_cols, 3 * inner),
        taps,
        first_pre,
        block_input,
        first_weight,
        fw,
    )
    fw = fw.reshape(count // 2, 2, own, LANES)
    kept, given = jnp.where(odd, fw[:, 1], fw[:, 0]), jnp.where(odd, fw[:, 0], fw[:, 1])
    fw = (kept + swap_cores(given, count)).astype(BF)
    got = exchange_chips(
        jnp.concatenate([jnp.broadcast_to(share[None], part.shape), fw], axis=1), count
    )
    first_wgrad = jnp.sum(got[:, size:].astype(F32), axis=0) * factor
    mine = got[:, :size].reshape(half, LANES)
    other = swap_cores(mine, count)
    both = jnp.where(
        odd, jnp.concatenate([other, mine]), jnp.concatenate([mine, other])
    ).astype(F32)
    middle_wgrad = both[: 9 * inner].reshape(3, 3, inner, inner)
    last_wgrad = (
        both[9 * inner :].reshape(-1, inner, LANES).transpose(1, 0, 2).reshape(inner, channels)
    )
    return (buf, first_wgrad, middle_wgrad, last_wgrad)


def solution(mesh):
    placed = (
        P(("groups", "rows"), None, None),
        P(("groups", "rows"), None, None),
        P(("groups", "rows"), None, None),
        P(("groups", "rows"), None, None),
        P("groups", None, "rows"),
        P(),
        P(),
        P(),
    )
    return jax.shard_map(
        shards,
        mesh=mesh,
        in_specs=placed,
        out_specs=(
            P(("groups", "rows"), None, None),
            P(("groups", "rows"), None),
            P("groups", None, None, None),
            P("groups", None),
        ),
        check_vma=False,
    )
```

time: 230 us -> 214 us (0.930)
  starting transfers between devices: 61.7 us -> 45.1 us
  blocking collectives: 0 us -> 16.2 us
  waiting for transfers between devices: 87.9 us -> 75.9 us
  other arithmetic: 9.31 us -> 5.72 us
    all_to_all x0 -> x1, blocking collectives: none -> 16.2 us  [exchange_chips(): lax.all_to_all(value, AXIS, 0, 0, tiled=True, axis_index_groups=same_core)]
    all_to_all x5 -> x3, starting transfers between devices: 49 us -> 36.8 us  [the longest x2 27.3 us: exchange(): return lax.all_to_all(value, AXIS, 0, 0, tiled=True)]
    all_to_all x5 -> x3, waiting for transfers between devices: 82.5 us -> 71.5 us  [the longest x2 71.5 us: exchange(): return lax.all_to_all(value, AXIS, 0, 0, tiled=True)]
    ppermute x3 -> x1, starting transfers between devices: 7.05 us -> 3.3 us  [edges(): lax.ppermute(value[-1:], AXIS, up)]
    pallas_call x2, Pallas kernels: 19 us -> 15.8 us  [open_block(): return call(*((buf,) + args if alias else args))]
    ppermute x3 -> x1, waiting for transfers between devices: 2.62 us -> 0.01 us  [edges(): lax.ppermute(value[:1], AXIS, down)]
    ppermute x3 -> x1, starting transfers between devices: 3.88 us -> 1.28 us  [edges(): lax.ppermute(value[:1], AXIS, down)]
    pallas_call x2, Pallas kernels: 6.98 us -> 9.57 us  [pack(): pl.pallas_call(functools.partial(pack_kernel, tile_rows, u, groups), grid...]
  transfers between devices with their start and end apart: 14 -> 8, of which waited for: 7 -> 6; matrix products, arithmetic and copies ran while one was open for 6% -> 5% of each run, Pallas kernels for 16% -> 17%
where the time goes in v2:
time: 214 us; the launch traced here: 213 us
  waiting for transfers between devices  75.9 us (35%)
  Pallas kernels  49.2 us (23%)
  starting transfers between devices  45.1 us (21%)
  local copies, waits for them, and re-layouts  19.5 us (9%)
  blocking collectives  16.2 us (8%)
  other arithmetic  5.72 us (3%)
    all_to_all x2, waiting for transfers between devices, exchange(): return lax.all_to_all(value, AXIS, 0, 0, tiled=True)  71.5 us
    all_to_all x2, starting transfers between devices, exchange(): return lax.all_to_all(value, AXIS, 0, 0, tiled=True)  27.3 us
    all_to_all x1, blocking collectives, exchange_chips(): lax.all_to_all(value, AXIS, 0, 0, tiled=True, axis_index_groups=same_core)  16.2 us
    pallas_call x2, Pallas kernels, open_block(): return call(*((buf,) + args if alias else args))  15.8 us
    pallas_call x2, Pallas kernels, close_block(): pl.pallas_call(functools.partial(close_kernel, u), grid=(blocks // u,), i...  15.6 us
    unnamed x43, local copies, waits for them, and re-layouts  12.2 us
    pallas_call x2, Pallas kernels, pack(): pl.pallas_call(functools.partial(pack_kernel, tile_rows, u, groups), grid...  9.57 us
    all_to_all x1, starting transfers between devices, exchange_chips(): lax.all_to_all(value, AXIS, 0, 0, tiled=True, axis_index_groups=same_core)  9.52 us
  transfers between devices with their start and end apart: 8, of which 6 were waited for; matrix products, arithmetic and copies ran while one was open for 5% of the time, Pallas kernels for 17%

profile of v2, /device:TPU:0, one launch (start us, length us, event | category | flops | bytes accessed | tf_op | source)
XLA Modules:
  0.0 212.6 jit_solution(10948710347932576191)
XLA Ops:
  0.7 5.6 %pack.2 = bf16[16,16,64,128]{3,2,1,0:T(8,128)(2,1)} custom-call(bf16[11264,256]{1,0:T(8,128)(2,1)} %bitcast.42, bf16[256,256]{1,0:T(8,128)(2,1)S(1)} %fusion.20.eye_ref), custom_call_target="tpu_custom_call" | custom-call | flops 16777216 | bytes 131072 | tf_op jit(solution)/shard_map/pack/pallas_call | solution.py:82
  6.3 7.6 %all-to-all-start = ((bf16[16,16,64,128]{3,2,1,0:T(8,128)(2,1)}), bf16[16,16,64,128]{3,2,1,0:T(8,128)(2,1)}, u32[]{:S(2)}, u32[]{:S(2)}) async-start(bf16[16,16,64,128]{3,2,1,0:T(8,128)(2,1)} %pack.2), calls=%async_computation | async-start | bytes 8388608 | tf_op jit(solution)/shard_map/all_to_all | solution.py:385
  16.8 2.4 %slice.139.act = bf16[18,256,384]{2,1,0:T(8,128)(2,1)} slice(bf16[18,352,384]{2,1,0:T(8,128)(2,1)S(1)} %pad_maximum_fusion), slice={[0:18], [0:256], [0:384]} | slice | bytes 7077888 | tf_op jit(solution)/shard_map/slice | solution.py:456
  19.2 1.2 copy.26
  20.4 3.9 %pack.3 = bf16[16,6,64,128]{3,2,1,0:T(8,128)(2,1)} custom-call(bf16[11264,256]{1,0:T(8,128)(2,1)} %bitcast.43, bf16[256,256]{1,0:T(8,128)(2,1)S(1)} %fusion.20.eye_ref), custom_call_target="tpu_custom_call" | custom-call | flops 6291456 | bytes 49152 | tf_op jit(solution)/shard_map/pack/pallas_call | solution.py:82
  25.5 66.1 %all-to-all-done.refs_0_ = bf16[16,16,64,128]{3,2,1,0:T(8,128)(2,1)} async-done(((bf16[16,16,64,128]{3,2,1,0:T(8,128)(2,1)}), bf16[16,16,64,128]{3,2,1,0:T(8,128)(2,1)}, u32[]{:S(2)}, u32[]{:S(2)}) %all-to-all-start) | async-done | bytes 4194336 | tf_op jit(solution)/shard_map/all_to_all | solution.py:385
  91.6 19.7 %all-to-all-start.1 = ((bf16[16,6,64,128]{3,2,1,0:T(8,128)(2,1)}), bf16[16,6,64,128]{3,2,1,0:T(8,128)(2,1)}, u32[]{:S(2)}, u32[]{:S(2)}) async-start(bf16[16,6,64,128]{3,2,1,0:T(8,128)(2,1)} %pack.3), calls=%async_computation.1 | async-start | bytes 3145728 | tf_op jit(solution)/shard_map/all_to_all | solution.py:385
  111.3 10.1 %open_block.2 = (bf16[16,352,512]{2,1,0:T(8,128)(2,1)}, bf16[16,256,128]{2,1,0:T(8,128)(2,1)S(1)}, f32[4,128,128]{2,1,0:T(8,128)S(1)}) custom-call(bf16[16,16,64,128]{3,2,1,0:T(8,128)(2,1)} %all-to-all-done.refs_0_, bf16[16,352,512]{2,1,0:T(8,128)(2,1)} %refs_2_.3, bf16[16,352,128]{2,1,0:T(8,128)(2,1)} %refs_3_.1, ...), custom_call_target="tpu_custom_call" | custom-call | flops 67108864 | bytes 229376 | tf_op jit(solution)/shard_map/open_block/pallas_call | solution.py:197
  122.2 3.0 %middle.2.start_ref = f32[3,128,384]{2,1,0:T(8,128)S(1)} custom-call(bf16[16,256,128]{2,1,0:T(8,128)(2,1)S(1)} %get-tuple-element.40.sg, bf16[18,256,384]{2,1,0:T(8,128)(2,1)S(1)} %copy-done, f32[3,128,384]{2,1,0:T(8,128)S(1)} %broadcast_in_dim.9.start_ref), custom_call_target="tpu_custom_call" | custom-call | flops 18874368 | bytes 65536 | tf_op jit(solution)/shard_map/middle/pallas_call | solution.py:239
  126.9 9.6 %close_block.2 = (bf16[16,352,512]{2,1,0:T(8,128)(2,1)}, f32[128,512]{1,0:T(8,128)S(1)}) custom-call(bf16[16,352,512]{2,1,0:T(8,128)(2,1)} %get-tuple-element.39.buf_in, bf16[16,224,384]{2,1,0:T(8,128)(2,1)S(1)} %pad_maximum_fusion.1.sg, bf16[3,384,128]{2,1,0:T(8,128)(2,1)S(1)} %bitcast.37, ...), custom_call_target="tpu_custom_call", output_to_operand_aliasing={{0}: (0, {})} | custom-call | flops 31195136 | bytes 229376 | tf_op jit(solution)/shard_map/close_block/pallas_call | solution.py:301
  137.9 5.4 %all-to-all-done.1.refs_1_ = bf16[16,6,64,128]{3,2,1,0:T(8,128)(2,1)} async-done(((bf16[16,6,64,128]{3,2,1,0:T(8,128)(2,1)}), bf16[16,6,64,128]{3,2,1,0:T(8,128)(2,1)}, u32[]{:S(2)}, u32[]{:S(2)}) %all-to-all-start.1) | async-done | bytes 1572896 | tf_op jit(solution)/shard_map/all_to_all | solution.py:385
  145.1 5.7 %open_block.3 = (bf16[16,352,512]{2,1,0:T(8,128)(2,1)}, bf16[16,96,128]{2,1,0:T(8,128)(2,1)S(1)}, f32[4,128,128]{2,1,0:T(8,128)S(1)}) custom-call(bf16[16,352,512]{2,1,0:T(8,128)(2,1)} %get-tuple-element.43.refs_0_, bf16[16,6,64,128]{3,2,1,0:T(8,128)(2,1)} %all-to-all-done.1.refs_1_, bf16[16,352,512]{2,1,0:T(8,128)(2,1)} %refs_2_.3, ...), custom_call_target="tpu_custom_call", output_to_operand_aliasing={{0}: (0, {})} | custom-call | flops 25165824 | bytes 86016 | tf_op jit(solution)/shard_map/open_block/pallas_call | solution.py:197
  152.3 1.3 collective-permute-start.1
  153.6 3.3 %collective-permute-start = (bf16[1,352,128]{2,1,0:T(8,128)(2,1)S(1)}, bf16[1,352,128]{2,1,0:T(8,128)(2,1)S(1)}, u32[]{:S(2)}, u32[]{:S(2)}) collective-permute-start(bf16[1,352,128]{2,1,0:T(8,128)(2,1)S(1)} %pad_maximum_fusion.7), channel_id=1, source_target_pairs={{0,1},{1,2},{2,3},{3,4},{4,5},{5,6},{6,7},{7,8},{8,9},{9,10},{10,1... | collective-permute-start | bytes 270344 | tf_op jit(solution)/shard_map/ppermute | solution.py:400
  158.8 1.1 copy-done.4
  159.9 1.0 copy-done.5
  161.9 1.7 middle.3
  163.7 3.6 %collective-permute-start.2 = (f32[832,128]{1,0:T(8,128)S(1)}, f32[832,128]{1,0:T(8,128)S(1)}, u32[]{:S(2)}, u32[]{:S(2)}) collective-permute-start(f32[832,128]{1,0:T(8,128)S(1)} %slice_select_fusion), channel_id=1, source_target_pairs={{0,1},{1,0},{2,3},{3,2},{4,5},{5,4},{6,7},{7,6},{8,9},{9,8},{10,11... | collective-permute-start | bytes 1277960 | tf_op jit(solution)/shard_map/ppermute | solution.py:394
  167.3 1.3 collective-permute-done.2
  169.8 9.5 %all-to-all-start.2 = ((bf16[8,104,128]{2,1,0:T(8,128)(2,1)}), bf16[8,104,128]{2,1,0:T(8,128)(2,1)S(1)}, u32[]{:S(2)}, u32[]{:S(2)}) async-start(bf16[8,104,128]{2,1,0:T(8,128)(2,1)} %bitcast.5), calls=%async_computation.2 | async-start | bytes 425984 | tf_op jit(solution)/shard_map/all_to_all | solution.py:390
  180.8 6.0 %close_block.3 = (bf16[16,352,512]{2,1,0:T(8,128)(2,1)}, f32[128,512]{1,0:T(8,128)S(1)}) custom-call(bf16[16,352,512]{2,1,0:T(8,128)(2,1)} %get-tuple-element.50.buf_in, bf16[16,128,384]{2,1,0:T(8,128)(2,1)S(1)} %pad_maximum_fusion.3.sg, bf16[3,384,128]{2,1,0:T(8,128)(2,1)S(1)} %bitcast.38, ...), custom_call_target="tpu_custom_call", output_to_operand_aliasing={{0}: (0, {})} | custom-call | flops 17825792 | bytes 131072 | tf_op jit(solution)/shard_map/close_block/pallas_call | solution.py:301
  187.9 3.5 %close_edges.1 = (bf16[16,352,512]{2,1,0:T(8,128)(2,1)}, f32[512,128]{1,0:T(8,128)S(1)}) custom-call(bf16[16,352,512]{2,1,0:T(8,128)(2,1)} %get-tuple-element.59.buf_in, bf16[2,3,352,384]{3,2,1,0:T(8,128)(2,1)S(1)} %bitcast.36, bf16[3,384,128]{2,1,0:T(8,128)(2,1)S(1)} %bitcast.39, bf16[16,352,128]{2,1,0:T(8,128)(2,1)} %fpre.2, ...), custom_call_target="tpu_custom_call", output_to_operand_aliasing={{0}: (0, {})} | custom-call | flops 6127616 | bytes 33792 | tf_op jit(solution)/shard_map/close_edges/pallas_call | solution.py:357
  191.5 1.3 collective-permute-done.3
  193.0 16.2 %all_to_all.20 = bf16[8,136,128]{2,1,0:T(8,128)(2,1)S(1)} all-to-all(bf16[8,136,128]{2,1,0:T(8,128)(2,1)S(1)} %pad_maximum_fusion.5), channel_id=1, replica_groups={{0,2,4,6,8,10,12,14},{1,3,5,7,9,11,13,15},{16,18,20,22,24,26,28,30},{17..., dimensions={0} | all-to-all | bytes 557056 | tf_op jit(solution)/shard_map/all_to_all | solution.py:390
  (92 shorter events, 21.5 us)
Async XLA Ops:
  6.3 7.6 %copy-start.15 = (bf16[16,352,128]{2,1,0:T(8,128)(2,1)S(1)}, bf16[16,352,128]{2,1,0:T(8,128)(2,1)}, u32[]{:S(2)}) copy-start(bf16[16,352,128]{2,1,0:T(8,128)(2,1)} %fpre.2) | copy-start | bytes 4325380
  6.3 85.2 %all-to-all-start = ((bf16[16,16,64,128]{3,2,1,0:T(8,128)(2,1)}), bf16[16,16,64,128]{3,2,1,0:T(8,128)(2,1)}, u32[]{:S(2)}, u32[]{:S(2)}) async-start(bf16[16,16,64,128]{3,2,1,0:T(8,128)(2,1)} %pack.2), calls=%async_computation | async-start | bytes 8388608 | tf_op jit(solution)/shard_map/all_to_all | solution.py:385
  14.9 1.2 copy-start.16
  14.9 1.8 copy-start.18
  20.3 4.0 %copy-start.17 = (bf16[18,352,128]{2,1,0:T(8,128)(2,1)S(1)}, bf16[18,352,128]{2,1,0:T(8,128)(2,1)}, u32[]{:S(2)}) copy-start(bf16[18,352,128]{2,1,0:T(8,128)(2,1)} %copy-done.16) | copy-start | bytes 4866052
  20.3 4.0 %copy-start.19 = (bf16[18,352,128]{2,1,0:T(8,128)(2,1)S(1)}, bf16[18,352,128]{2,1,0:T(8,128)(2,1)}, u32[]{:S(2)}) copy-start(bf16[18,352,128]{2,1,0:T(8,128)(2,1)} %copy-done.18) | copy-start | bytes 4866052
  25.5 85.8 %copy-start.7 = (bf16[128,512]{1,0:T(8,128)(2,1)S(1)}, bf16[128,512]{1,0:T(8,128)(2,1)}, u32[]{:S(2)}) copy-start(bf16[128,512]{1,0:T(8,128)(2,1)} %refs_6_.1) | copy-start | bytes 393220
  91.6 51.7 %all-to-all-start.1 = ((bf16[16,6,64,128]{3,2,1,0:T(8,128)(2,1)}), bf16[16,6,64,128]{3,2,1,0:T(8,128)(2,1)}, u32[]{:S(2)}, u32[]{:S(2)}) async-start(bf16[16,6,64,128]{3,2,1,0:T(8,128)(2,1)} %pack.3), calls=%async_computation.1 | async-start | bytes 3145728 | tf_op jit(solution)/shard_map/all_to_all | solution.py:385
  111.3 10.9 %copy-start = (bf16[18,256,384]{2,1,0:T(8,128)(2,1)S(1)}, bf16[18,256,384]{2,1,0:T(8,128)(2,1)}, u32[]{:S(2)}) copy-start(bf16[18,256,384]{2,1,0:T(8,128)(2,1)} %slice.139.act) | copy-start | bytes 10616836
  126.0 0.9 copy-start.6
  143.3 0.9 copy-start.8
  144.2 0.9 copy-start.10
  145.1 8.4 %copy-start.20 = (bf16[1,256,128]{2,1,0:T(8,128)(2,1)S(1)}, bf16[1,256,128]{2,1,0:T(8,128)(2,1)}, u32[]{:S(2)}) copy-start(bf16[1,256,128]{2,1,0:T(8,128)(2,1)} %get-tuple-element.73) | copy-start | bytes 196612
  152.3 4.6 %collective-permute-start.1 = (bf16[1,352,128]{2,1,0:T(8,128)(2,1)S(1)}, bf16[1,352,128]{2,1,0:T(8,128)(2,1)S(1)}, u32[]{:S(2)}, u32[]{:S(2)}) collective-permute-start(bf16[1,352,128]{2,1,0:T(8,128)(2,1)S(1)} %pad_maximum_fusion.8), channel_id=1, source_target_pairs={{1,0},{2,1},{3,2},{4,3},{5,4},{6,5},{7,6},{8,7},{9,8},{10,9},{11,1... | collective-permute-start | bytes 270344 | tf_op jit(solution)/shard_map/ppermute | solution.py:400
  153.6 4.2 %collective-permute-start = (bf16[1,352,128]{2,1,0:T(8,128)(2,1)S(1)}, bf16[1,352,128]{2,1,0:T(8,128)(2,1)S(1)}, u32[]{:S(2)}, u32[]{:S(2)}) collective-permute-start(bf16[1,352,128]{2,1,0:T(8,128)(2,1)S(1)} %pad_maximum_fusion.7), channel_id=1, source_target_pairs={{0,1},{1,2},{2,3},{3,4},{4,5},{5,6},{6,7},{7,8},{8,9},{9,10},{10,1... | collective-permute-start | bytes 270344 | tf_op jit(solution)/shard_map/ppermute | solution.py:400
  157.8 1.0 copy-start.2
  158.8 1.1 copy-start.4
  159.9 1.0 copy-start.5
  160.9 0.9 copy-start.12
  163.7 5.0 %collective-permute-start.2 = (f32[832,128]{1,0:T(8,128)S(1)}, f32[832,128]{1,0:T(8,128)S(1)}, u32[]{:S(2)}, u32[]{:S(2)}) collective-permute-start(f32[832,128]{1,0:T(8,128)S(1)} %slice_select_fusion), channel_id=1, source_target_pairs={{0,1},{1,0},{2,3},{3,2},{4,5},{5,4},{6,7},{7,6},{8,9},{9,8},{10,11... | collective-permute-start | bytes 1277960 | tf_op jit(solution)/shard_map/ppermute | solution.py:394
  169.8 23.0 %all-to-all-start.2 = ((bf16[8,104,128]{2,1,0:T(8,128)(2,1)}), bf16[8,104,128]{2,1,0:T(8,128)(2,1)S(1)}, u32[]{:S(2)}, u32[]{:S(2)}) async-start(bf16[8,104,128]{2,1,0:T(8,128)(2,1)} %bitcast.5), calls=%async_computation.2 | async-start | bytes 425984 | tf_op jit(solution)/shard_map/all_to_all | solution.py:390
  179.9 1.0 copy-start.14
  191.4 1.4 collective-permute-start.3
  209.1 1.5 collective-permute-start.4
  (5 other events, 3.7 us)

commit v3 on v2

--- a/solution.py
+++ b/solution.py
@@ -32,9 +32,7 @@
 
 
 def params():
-    return pltpu.CompilerParams(
-        dimension_semantics=("arbitrary",), vmem_limit_bytes=24 * 2**20
-    )
+    return pltpu.CompilerParams(vmem_limit_bytes=24 * 2**20)
 
 
 def hbm(value):
@@ -58,39 +56,67 @@
     return (a == b).astype(BF)
 
 
-def pack_kernel(tile_rows, units, groups, x_ref, eye_ref, out_ref):
+def pack_kernel(tile_rows, groups, start, x, eye_ref, out, held, ready, came, gone):
     side = eye_ref.shape[0]
     per = side // tile_rows
+    steps, count, units = ready.shape[:3]
     depth = groups * LANES
-    for u in range(units):
-        for h in range(x_ref.shape[1] // side):
-            part = x_ref[u * depth : (u + 1) * depth, h * side : (h + 1) * side]
-            turned = mm_nt(eye_ref[...], part).astype(BF)
-            for g in range(groups):
-                piece = turned[:, g * LANES : (g + 1) * LANES]
-                out_ref[
-                    h * per : (h + 1) * per, u, g * tile_rows : (g + 1) * tile_rows, :
-                ] = piece.reshape(per, tile_rows, LANES)
+    size = units * depth
+    loads = [
+        pltpu.make_async_copy(
+            x.at[pl.ds(start * depth + k * size, size), :], held.at[k], came.at[k]
+        )
+        for k in range(steps)
+    ]
+    stores = [
+        pltpu.make_async_copy(
+            ready.at[k], out.at[:, pl.ds(k * units, units), :, :], gone.at[k]
+        )
+        for k in range(steps)
+    ]
+    for load in loads:
+        load.start()
+    for k in range(steps):
+        loads[k].wait()
+        for u in range(units):
+            for h in range(held.shape[2] // side):
+                part = held[
+                    k, u * depth : (u + 1) * depth, h * side : (h + 1) * side
+                ]
+                turned = mm_nt(eye_ref[...], part).astype(BF)
+                for g in range(groups):
+                    piece = turned[:, g * LANES : (g + 1) * LANES]
+                    ready[
+                        k,
+                        h * per : (h + 1) * per,
+                        u,
+                        g * tile_rows : (g + 1) * tile_rows,
+                        :,
+                    ] = piece.reshape(per, tile_rows, LANES)
+        stores[k].start()
+    for store in stores:
+        store.wait()
 
 
 def pack(x, count, tile_rows, groups, start, blocks):
     depth = groups * LANES
     height = x.shape[1]
     side = 256 if height % 256 == 0 else LANES
-    u = unit(blocks, start, 4)
-    first = start // u
+    u = unit(blocks, 0, 2)
+    steps = blocks // u
+    anywhere = lambda: pl.BlockSpec(memory_space=pltpu.HBM)
     return pl.pallas_call(
-        functools.partial(pack_kernel, tile_rows, u, groups),
-        grid=(blocks // u,),
-        in_specs=[
-            pl.BlockSpec((u * depth, height), lambda i: (first + i, 0)),
-            whole((side, side)),
-        ],
-        out_specs=pl.BlockSpec(
-            (count, u, groups * tile_rows, LANES), lambda i: (0, i, 0, 0)
-        ),
+        functools.partial(pack_kernel, tile_rows, groups, start),
+        in_specs=[anywhere(), pl.BlockSpec(memory_space=pltpu.VMEM)],
+        out_specs=anywhere(),
         out_shape=pltpu.HBM((count, blocks, groups * tile_rows, LANES), BF),
-        compiler_params=params(),
+        scratch_shapes=[
+            pltpu.VMEM((steps, u * depth, height), BF),
+            pltpu.VMEM((steps, count, u, groups * tile_rows, LANES), BF),
+            pltpu.SemaphoreType.DMA((steps,)),
+            pltpu.SemaphoreType.DMA((steps,)),
+        ],
+        compiler_params=pltpu.CompilerParams(vmem_limit_bytes=24 * 2**20),
         cost_estimate=cost(
             2 * height * side * blocks * depth, 4 * blocks * depth * height
         ),
@@ -120,7 +146,6 @@
         axis=0,
     )
     sorted_lanes = mm(stack, lanes_ref[...]).astype(BF)
-    spatial = []
     for u in range(units):
         by_pixel = jnp.concatenate(
             [
@@ -138,13 +163,11 @@
             ],
             axis=0,
         )
-        spatial.append(
-            mm(pixels_ref[...], by_pixel).reshape(rows, BLK, tiles * LANES)
-        )
-    spatial = jnp.concatenate(spatial, axis=1).reshape(pixels, tiles * LANES)
-    gate = opre[...].reshape(pixels, tiles * LANES).astype(F32) > 0
-    masked = jnp.where(gate, spatial, 0.0).astype(BF)
-    buf[...] = masked.reshape(buf.shape)
+        spatial = mm(pixels_ref[...], by_pixel).reshape(rows, BLK, tiles * LANES)
+        cols = slice(u * BLK, (u + 1) * BLK)
+        gate = opre[:, cols, :].astype(F32) > 0
+        buf[:, cols, :] = jnp.where(gate, spatial, 0.0).astype(BF)
+    masked = buf[...].reshape(pixels, tiles * LANES)
     pre = spre[...].reshape(pixels, LANES).astype(F32)
     inner = mm_nt(masked, weight[...])
     sg[...] = jnp.where(pre > 0, inner, 0.0).astype(BF).reshape(sg.shape)
@@ -184,7 +207,7 @@
         out_shape=[
             jax.ShapeDtypeStruct(opre.shape, BF),
             jax.ShapeDtypeStruct((rows, blocks * BLK, LANES), BF),
-            jax.ShapeDtypeStruct(lw_in.shape, F32),
+            (jax.ShapeDtypeStruct if alias else pltpu.HBM)(lw_in.shape, F32),
         ],
         input_output_aliases={0: 0} if alias else {},
         compiler_params=params(),
@@ -193,49 +216,30 @@
         ),
         name="open_block",
     )
-    args = (hbm(recv), hbm(opre), hbm(spre), lane_sort, pixel_sort, weight, lw_in)
+    args = (recv if alias else hbm(recv),) + tuple(
+        hbm(v) for v in (opre, spre, lane_sort, pixel_sort, weight, lw_in)
+    )
     return call(*(((buf,) + args) if alias else args))
 
 
-def middle_kernel(units, sg, act, start_ref, *refs):
-    lw, rim, rim_act, out, total = refs if len(refs) == 5 else (None,) * 3 + refs
-    step = pl.program_id(0)
+def middle_kernel(units, sg, act, start_ref, out):
     rows = sg.shape[0]
     pixels = rows * units * BLK
 
-    @pl.when(step == 0)
+    @pl.when(pl.program_id(0) == 0)
     def _():
-        total[...] = start_ref[...]
+        out[...] = start_ref[...]
 
     turned = jnp.transpose(sg[...].reshape(pixels, LANES))
     for a in range(3):
         window = act[a : a + rows].reshape(pixels, 3 * LANES)
-        total[a] += mm(turned, window)
-
-    @pl.when(step == pl.num_programs(0) - 1)
-    def _():
-        if lw is None:
-            out[...] = total[...]
-        else:
-            for e in range(2):
-                total[2 - 2 * e] += mm(jnp.transpose(rim[e]), rim_act[e])
-            for a in range(3):
-                for b in range(3):
-                    top = (3 * a + b) * LANES
-                    out[top : top + LANES, :] = jnp.transpose(
-                        total[a, :, b * LANES : (b + 1) * LANES]
-                    )
-            for t in range(lw.shape[0]):
-                top = (9 + t) * LANES
-                out[top : top + LANES, :] = lw[t]
-
-
-def middle(sg, act, start, lw=None, rim=None, rim_act=None):
+        out[a] += mm(turned, window)
+
+
+def middle(sg, act, start):
     rows, width, _ = sg.shape
     blocks = width // BLK
     u = unit(blocks, 0, 4)
-    extra = () if lw is None else (lw, rim, rim_act)
-    shape = start.shape if lw is None else ((9 + lw.shape[0]) * LANES, LANES)
     return pl.pallas_call(
         functools.partial(middle_kernel, u),
         grid=(blocks // u,),
@@ -243,17 +247,43 @@
             pl.BlockSpec((rows, u * BLK, LANES), lambda i: (0, i, 0)),
             pl.BlockSpec((rows + 2, u * BLK, 3 * LANES), lambda i: (0, i, 0)),
             whole(start.shape),
-        ]
-        + [whole(e.shape) for e in extra],
-        out_specs=whole(shape),
-        out_shape=jax.ShapeDtypeStruct(shape, F32),
-        scratch_shapes=[pltpu.VMEM((3, LANES, 3 * LANES), F32)],
+        ],
+        out_specs=whole(start.shape),
+        out_shape=jax.ShapeDtypeStruct(start.shape, F32),
         compiler_params=params(),
         cost_estimate=cost(
             2 * rows * width * 9 * LANES * LANES, rows * width * 2 * 4 * LANES
         ),
         name="middle",
-    )(sg, act, start, *extra)
+    )(sg, act, start)
+
+
+def rim_kernel(mw, lw, before, after, act, out):
+    sums = [mw[a] for a in range(3)]
+    sums[2] += mm(jnp.transpose(before[...]), act[0])
+    sums[0] += mm(jnp.transpose(after[...]), act[1])
+    for a in range(3):
+        for b in range(3):
+            top = (3 * a + b) * LANES
+            out[top : top + LANES, :] = jnp.transpose(
+                sums[a][:, b * LANES : (b + 1) * LANES]
+            )
+    for t in range(lw.shape[0]):
+        top = (9 + t) * LANES
+        out[top : top + LANES, :] = lw[t]
+
+
+def add_rims(mw, lw, before, after, act):
+    space = pl.BlockSpec(memory_space=pltpu.VMEM)
+    return pl.pallas_call(
+        rim_kernel,
+        in_specs=[space] * 5,
+        out_specs=space,
+        out_shape=jax.ShapeDtypeStruct(((9 + lw.shape[0]) * LANES, LANES), F32),
+        compiler_params=params(),
+        cost_estimate=cost(2**20, 2**20),
+        name="add_rims",
+    )(mw, lw, before, after, act)
 
 
 def add_pixels(moved, taps, fpre, binput, weight, direct, total):
@@ -313,7 +343,7 @@
         out_specs=[wide(channels), whole(fw_in.shape)],
         out_shape=[
             jax.ShapeDtypeStruct(buf.shape, BF),
-            jax.ShapeDtypeStruct(fw_in.shape, F32),
+            pltpu.HBM(fw_in.shape, F32),
         ],
         input_output_aliases={0: 0},
         compiler_params=params(),
@@ -322,7 +352,7 @@
             2 * pixels * (3 * channels + 4 * LANES),
         ),
         name="close_block",
-    )(buf, sg, taps, hbm(fpre), hbm(binput), weight, fw_in)
+    )(buf, sg, hbm(taps), hbm(fpre), hbm(binput), hbm(weight), hbm(fw_in))
 
 
 def edge_kernel(buf_in, sg, taps, fpre, binput, weight, fw_in, buf, fw, total):
@@ -378,7 +408,49 @@
             4 * width * LANES * (9 * LANES + 2 * channels), 12 * width * channels
         ),
         name="close_edges",
-    )(buf, sg, taps, hbm(fpre), hbm(binput), weight, fw_in)
+    )(buf, sg, hbm(taps), hbm(fpre), hbm(binput), hbm(weight), hbm(fw_in))
+
+
+def finish_kernel(size, factor, odd_ref, mine, other, mw, lw, fw):
+    chips = mine.shape[0]
+    odd = odd_ref[0] == 1
+    top = mw.shape[0]
+    for h in range(2):
+        for k in range(chips):
+            a, b = mine[k, :size, :].astype(F32), other[k, :size, :].astype(F32)
+            value = jnp.where(odd, a if h else b, b if h else a)
+            start = (h * chips + k) * size
+            at = start
+            while at < start + size:
+                stop = min(start + size, (at // LANES + 1) * LANES)
+                piece = value[at - start : stop - start]
+                if at < top:
+                    mw[at:stop, :] = piece
+                else:
+                    t, m = divmod(at - top, LANES)
+                    lw[m : m + stop - at, t * LANES : (t + 1) * LANES] = piece
+                at = stop
+    total = mine[0, size:, :].astype(F32)
+    for k in range(1, chips):
+        total = total + mine[k, size:, :].astype(F32)
+    fw[...] = total * factor
+
+
+def finish(odd, mine, other, size, factor, inner, channels):
+    own = mine.shape[1] - size
+    space = lambda: pl.BlockSpec(memory_space=pltpu.VMEM)
+    return pl.pallas_call(
+        functools.partial(finish_kernel, size, factor),
+        in_specs=[pl.BlockSpec(memory_space=pltpu.SMEM), space(), space()],
+        out_specs=[space(), space(), space()],
+        out_shape=[
+            jax.ShapeDtypeStruct((9 * inner, LANES), F32),
+            jax.ShapeDtypeStruct((inner, channels), F32),
+            jax.ShapeDtypeStruct((own, LANES), F32),
+        ],
+        compiler_params=pltpu.CompilerParams(vmem_limit_bytes=24 * 2**20),
+        name="finish",
+    )(odd, mine, other)
 
 
 def exchange(value):
@@ -394,10 +466,14 @@
     return lax.ppermute(value, AXIS, [(i, i ^ 1) for i in range(count)])
 
 
-def edges(value, count):
-    up = [(i, i + 1) for i in range(count - 1)]
-    down = [(i + 1, i) for i in range(count - 1)]
-    return lax.ppermute(value[-1:], AXIS, up), lax.ppermute(value[:1], AXIS, down)
+def edges(first, last, count):
+    odd = lax.axis_index(AXIS) % 2 == 1
+    near = swap_cores(jnp.where(odd, first, last), count)
+    pairs = [(i, i + 1) for i in range(1, count - 1, 2)]
+    across = lax.ppermute(
+        jnp.where(odd, last, first), AXIS, pairs + [(j, i) for i, j in pairs]
+    )
+    return jnp.where(odd, near, across), jnp.where(odd, across, near)
 
 
 def sorted_taps(ext, width):
@@ -487,17 +563,13 @@
     buf, sg_b, lw = open_block(
         buf, recv_b, output_pre, second_pre, *sorts, last_weight, lw, join, head
     )
-    rims = jnp.concatenate(
-        [
-            jnp.concatenate([sg_a[e : e + 1], sg_b[e : e + 1]], axis=1)
-            for e in (0, tile_rows - 1)
-        ],
-        axis=0,
-    )
-    before, after = edges(rims, count)
-    both = middle(
-        sg_b, act_b, mw, lw, jnp.concatenate([before, after], axis=0), rim_act
-    )
+    first, last = [
+        jnp.concatenate([sg_a[e : e + 1], sg_b[e : e + 1]], axis=1)
+        for e in (0, tile_rows - 1)
+    ]
+    before, after = edges(first, last, count)
+    mw = middle(sg_b, act_b, mw)
+    both = add_rims(mw, lw, before[0], after[0], rim_act)
 
     odd = lax.axis_index(AXIS) % 2 == 1
     half = both.shape[0] // 2
@@ -540,17 +612,11 @@
     got = exchange_chips(
         jnp.concatenate([jnp.broadcast_to(share[None], part.shape), fw], axis=1), count
     )
-    first_wgrad = jnp.sum(got[:, size:].astype(F32), axis=0) * factor
-    mine = got[:, :size].reshape(half, LANES)
-    other = swap_cores(mine, count)
-    both = jnp.where(
-        odd, jnp.concatenate([other, mine]), jnp.concatenate([mine, other])
-    ).astype(F32)
-    middle_wgrad = both[: 9 * inner].reshape(3, 3, inner, inner)
-    last_wgrad = (
-        both[9 * inner :].reshape(-1, inner, LANES).transpose(1, 0, 2).reshape(inner, channels)
-    )
-    return (buf, first_wgrad, middle_wgrad, last_wgrad)
+    other = swap_cores(got, count)
+    middle_wgrad, last_wgrad, first_wgrad = finish(
+        odd.astype(jnp.int32).reshape(1), got, other, size, factor, inner, channels
+    )
+    return (buf, first_wgrad, middle_wgrad.reshape(3, 3, inner, inner), last_wgrad)
 
 
 def solution(mesh):

time: 214 us -> 200 us (0.935)
  local copies, waits for them, and re-layouts: 19.5 us -> 9.47 us
  starting transfers between devices: 45.1 us -> 41.7 us
    unnamed x43 -> x12, local copies, waits for them, and re-layouts: 12.2 us -> 0.61 us
    ppermute x2 -> x1, starting transfers between devices: 4.58 us -> 0.85 us  [edges(): lax.ppermute(jnp.where(odd, last, first), AXIS, pairs + [(j, i) for i, j...]
    ppermute x3 -> x4, starting transfers between devices: 3.72 us -> 4.88 us  [swap_cores(): return lax.ppermute(value, AXIS, [(i, i ^ 1) for i in range(count)])]
    pallas_call x2 -> x4, Pallas kernels: 9.57 us -> 9.09 us  [the longest x2 7.68 us: pack(): pl.pallas_call(functools.partial(pack_kernel, tile_rows, groups, start),...]
  transfers between devices with their start and end apart: 8 -> 8, of which waited for: 6 -> 5; matrix products, arithmetic and copies ran while one was open for 5% -> 7% of each run, Pallas kernels for 17% -> 19%
where the time goes in v3:
time: 200 us; the launch traced here: 199 us
  waiting for transfers between devices  75 us (38%)
  Pallas kernels  49.1 us (25%)
  starting transfers between devices  41.7 us (21%)
  blocking collectives  16.2 us (8%)
  local copies, waits for them, and re-layouts  9.47 us (5%)
  other arithmetic  6.61 us (3%)
    all_to_all x2, waiting for transfers between devices, exchange(): return lax.all_to_all(value, AXIS, 0, 0, tiled=True)  70.8 us
    all_to_all x2, starting transfers between devices, exchange(): return lax.all_to_all(value, AXIS, 0, 0, tiled=True)  27.2 us
    pallas_call x2, Pallas kernels, close_block(): pl.pallas_call(functools.partial(close_kernel, u), grid=(blocks // u,), i...  16.2 us
    all_to_all x1, blocking collectives, exchange_chips(): lax.all_to_all(value, AXIS, 0, 0, tiled=True, axis_index_groups=same_core)  16.2 us
    pallas_call x2, Pallas kernels, open_block(): return call(*((buf,) + args if alias else args))  15.8 us
    all_to_all x1, starting transfers between devices, exchange_chips(): lax.all_to_all(value, AXIS, 0, 0, tiled=True, axis_index_groups=same_core)  8.78 us
    pallas_call x2, Pallas kernels, pack(): pl.pallas_call(functools.partial(pack_kernel, tile_rows, groups, start),...  7.68 us
    ppermute x4, starting transfers between devices, swap_cores(): return lax.ppermute(value, AXIS, [(i, i ^ 1) for i in range(count)])  4.88 us
  transfers between devices with their start and end apart: 8, of which 5 were waited for; matrix products, arithmetic and copies ran while one was open for 7% of the time, Pallas kernels for 19%

profile of v3, /device:TPU:0, one launch (start us, length us, event | category | flops | bytes accessed | tf_op | source)
XLA Modules:
  0.0 199.1 jit_solution(6154639417727051124)
XLA Ops:
  0.7 4.7 %pack.2 = bf16[16,16,64,128]{3,2,1,0:T(8,128)(2,1)} custom-call(bf16[11264,256]{1,0:T(8,128)(2,1)} %bitcast.35, bf16[256,256]{1,0:T(8,128)(2,1)S(1)} %fusion.19.eye_ref), custom_call_target="tpu_custom_call" | custom-call | flops 16777216 | bytes 131072 | tf_op jit(solution)/shard_map/pack/pallas_call | solution.py:108
  5.3 7.6 %all-to-all-start = ((bf16[16,16,64,128]{3,2,1,0:T(8,128)(2,1)}), bf16[16,16,64,128]{3,2,1,0:T(8,128)(2,1)}, u32[]{:S(2)}, u32[]{:S(2)}) async-start(bf16[16,16,64,128]{3,2,1,0:T(8,128)(2,1)} %pack.2), calls=%async_computation | async-start | bytes 8388608 | tf_op jit(solution)/shard_map/all_to_all | solution.py:457
  15.2 1.2 slice.124.act
  16.4 2.4 %slice.123.act = bf16[18,256,384]{2,1,0:T(8,128)(2,1)} slice(bf16[18,352,384]{2,1,0:T(8,128)(2,1)S(1)} %pad_maximum_fusion), slice={[0:18], [0:256], [0:384]} | slice | bytes 7077888 | tf_op jit(solution)/shard_map/slice | solution.py:532
  18.8 1.8 copy.17
  20.6 3.0 %pack.3 = bf16[16,6,64,128]{3,2,1,0:T(8,128)(2,1)} custom-call(bf16[11264,256]{1,0:T(8,128)(2,1)} %bitcast.36, bf16[256,256]{1,0:T(8,128)(2,1)S(1)} %fusion.19.eye_ref), custom_call_target="tpu_custom_call" | custom-call | flops 6291456 | bytes 49152 | tf_op jit(solution)/shard_map/pack/pallas_call | solution.py:108
  25.3 1.0 fusion.7.refs_3_.refs_4_
  26.3 64.3 %all-to-all-done.refs_0_ = bf16[16,16,64,128]{3,2,1,0:T(8,128)(2,1)} async-done(((bf16[16,16,64,128]{3,2,1,0:T(8,128)(2,1)}), bf16[16,16,64,128]{3,2,1,0:T(8,128)(2,1)}, u32[]{:S(2)}, u32[]{:S(2)}) %all-to-all-start) | async-done | bytes 4194336 | tf_op jit(solution)/shard_map/all_to_all | solution.py:457
  90.6 19.6 %all-to-all-start.1 = ((bf16[16,6,64,128]{3,2,1,0:T(8,128)(2,1)}), bf16[16,6,64,128]{3,2,1,0:T(8,128)(2,1)S(1)}, u32[]{:S(2)}, u32[]{:S(2)}) async-start(bf16[16,6,64,128]{3,2,1,0:T(8,128)(2,1)} %pack.3), calls=%async_computation.1 | async-start | bytes 3145728 | tf_op jit(solution)/shard_map/all_to_all | solution.py:457
  111.0 10.1 %open_block.2 = (bf16[16,352,512]{2,1,0:T(8,128)(2,1)}, bf16[16,256,128]{2,1,0:T(8,128)(2,1)S(1)}, f32[4,128,128]{2,1,0:T(8,128)}) custom-call(bf16[16,16,64,128]{3,2,1,0:T(8,128)(2,1)} %all-to-all-done.refs_0_, bf16[16,352,512]{2,1,0:T(8,128)(2,1)} %refs_2_.3, bf16[16,352,128]{2,1,0:T(8,128)(2,1)} %refs_3_.1, bf16[512,512]{1,0:T(8,128)(2,1)} %fusion.7.refs_3_.refs_4_, ...), custom_call_target="tpu_custom_call" | custom-call | flops 67108864 | bytes 229376 | tf_op jit(solution)/shard_map/open_block/pallas_call | solution.py:222
  121.2 3.0 %middle.2.start_ref = f32[3,128,384]{2,1,0:T(8,128)S(1)} custom-call(bf16[16,256,128]{2,1,0:T(8,128)(2,1)S(1)} %get-tuple-element.43.sg, bf16[18,256,384]{2,1,0:T(8,128)(2,1)S(1)} %copy-done, f32[3,128,384]{2,1,0:T(8,128)S(1)} %broadcast_in_dim.9.start_ref), custom_call_target="tpu_custom_call" | custom-call | flops 18874368 | bytes 65536 | tf_op jit(solution)/shard_map/middle/pallas_call | solution.py:243
  125.9 9.9 %close_block.2 = (bf16[16,352,512]{2,1,0:T(8,128)(2,1)}, f32[128,512]{1,0:T(8,128)}) custom-call(bf16[16,352,512]{2,1,0:T(8,128)(2,1)} %get-tuple-element.42.buf_in, bf16[16,224,384]{2,1,0:T(8,128)(2,1)S(1)} %pad_maximum_fusion.1.sg, bf16[3,384,128]{2,1,0:T(8,128)(2,1)} %bitcast.37, bf16[16,352,128]{2,1,0:T(8,128)(2,1)} %fpre.2, ...), custom_call_target="tpu_custom_call", output_to_operand_aliasing={{0}: (0, {})} | custom-call | flops 31195136 | bytes 229376 | tf_op jit(solution)/shard_map/close_block/pallas_call | solution.py:331
  135.8 6.5 %all-to-all-done.1.refs_1_ = bf16[16,6,64,128]{3,2,1,0:T(8,128)(2,1)S(1)} async-done(((bf16[16,6,64,128]{3,2,1,0:T(8,128)(2,1)}), bf16[16,6,64,128]{3,2,1,0:T(8,128)(2,1)S(1)}, u32[]{:S(2)}, u32[]{:S(2)}) %all-to-all-start.1) | async-done | bytes 1572896 | tf_op jit(solution)/shard_map/all_to_all | solution.py:457
  142.2 5.7 %open_block.3 = (bf16[16,352,512]{2,1,0:T(8,128)(2,1)}, bf16[16,96,128]{2,1,0:T(8,128)(2,1)S(1)}, f32[4,128,128]{2,1,0:T(8,128)S(1)}) custom-call(bf16[16,352,512]{2,1,0:T(8,128)(2,1)} %get-tuple-element.46.refs_0_, bf16[16,6,64,128]{3,2,1,0:T(8,128)(2,1)S(1)} %all-to-all-done.1.refs_1_, ...), custom_call_target="tpu_custom_call", output_to_operand_aliasing={{0}: (0, {})} | custom-call | flops 25165824 | bytes 86016 | tf_op jit(solution)/shard_map/open_block/pallas_call | solution.py:222
  148.8 4.1 %collective-permute-start = (bf16[1,352,128]{2,1,0:T(8,128)(2,1)S(1)}, bf16[1,352,128]{2,1,0:T(8,128)(2,1)S(1)}, u32[]{:S(2)}, u32[]{:S(2)}) collective-permute-start(bf16[1,352,128]{2,1,0:T(8,128)(2,1)S(1)} %get-tuple-element.91), channel_id=1, source_target_pairs={{0,1},{1,0},{2,3},{3,2},{4,5},{5,4},{6,7},{7,6},{8,9},{9,8},{10,11... | collective-permute-start | bytes 270344 | tf_op jit(solution)/shard_map/ppermute | solution.py:466
  152.9 1.3 middle.3.mw
  155.6 1.3 collective-permute-done.2
  158.1 8.8 %all-to-all-start.2 = ((bf16[8,104,128]{2,1,0:T(8,128)(2,1)}), bf16[8,104,128]{2,1,0:T(8,128)(2,1)S(1)}, u32[]{:S(2)}, u32[]{:S(2)}) async-start(bf16[8,104,128]{2,1,0:T(8,128)(2,1)} %bitcast.7), calls=%async_computation.2 | async-start | bytes 425984 | tf_op jit(solution)/shard_map/all_to_all | solution.py:462
  167.4 1.0 pad_maximum_fusion.2
  168.7 6.4 %close_block.3 = (bf16[16,352,512]{2,1,0:T(8,128)(2,1)}, f32[128,512]{1,0:T(8,128)}) custom-call(bf16[16,352,512]{2,1,0:T(8,128)(2,1)} %get-tuple-element.53.buf_in, bf16[16,128,384]{2,1,0:T(8,128)(2,1)S(1)} %pad_maximum_fusion.3.sg, bf16[3,384,128]{2,1,0:T(8,128)(2,1)} %bitcast.38, bf16[16,352,128]{2,1,0:T(8,128)(2,1)} %fpre.2, ...), custom_call_target="tpu_custom_call", output_to_operand_aliasing={{0}: (0, {})} | custom-call | flops 17825792 | bytes 131072 | tf_op jit(solution)/shard_map/close_block/pallas_call | solution.py:331
  175.0 3.7 %close_edges.1 = (bf16[16,352,512]{2,1,0:T(8,128)(2,1)}, f32[512,128]{1,0:T(8,128)S(1)}) custom-call(bf16[16,352,512]{2,1,0:T(8,128)(2,1)} %get-tuple-element.62.buf_in, bf16[2,3,352,384]{3,2,1,0:T(8,128)(2,1)S(1)} %bitcast.30, bf16[3,384,128]{2,1,0:T(8,128)(2,1)} %bitcast.39, bf16[16,352,128]{2,1,0:T(8,128)(2,1)} %fpre.2, ...), custom_call_target="tpu_custom_call", output_to_operand_aliasing={{0}: (0, {})} | custom-call | flops 6127616 | bytes 33792 | tf_op jit(solution)/shard_map/close_edges/pallas_call | solution.py:387
  178.9 1.3 collective-permute-done.3
  180.4 16.2 %all_to_all.20.mine = bf16[8,136,128]{2,1,0:T(8,128)(2,1)S(1)} all-to-all(bf16[8,136,128]{2,1,0:T(8,128)(2,1)S(1)} %pad_maximum_fusion.5), channel_id=1, replica_groups={{0,2,4,6,8,10,12,14},{1,3,5,7,9,11,13,15},{16,18,20,22,24,26,28,30},{17..., dimensions={0} | all-to-all | bytes 557056 | tf_op jit(solution)/shard_map/all_to_all | solution.py:462
  196.5 1.6 collective-permute-done.4.other
  (55 shorter events, 11.7 us)
Async XLA Ops:
  5.3 7.6 %copy-start.3 = (bf16[16,352,128]{2,1,0:T(8,128)(2,1)S(1)}, bf16[16,352,128]{2,1,0:T(8,128)(2,1)}, u32[]{:S(2)}) copy-start(bf16[16,352,128]{2,1,0:T(8,128)(2,1)} %fpre.2) | copy-start | bytes 4325380
  5.3 85.3 %all-to-all-start = ((bf16[16,16,64,128]{3,2,1,0:T(8,128)(2,1)}), bf16[16,16,64,128]{3,2,1,0:T(8,128)(2,1)}, u32[]{:S(2)}, u32[]{:S(2)}) async-start(bf16[16,16,64,128]{3,2,1,0:T(8,128)(2,1)} %pack.2), calls=%async_computation | async-start | bytes 8388608 | tf_op jit(solution)/shard_map/all_to_all | solution.py:457
  13.9 1.3 copy-start.4
  20.6 3.1 %copy-start.5 = (bf16[18,352,128]{2,1,0:T(8,128)(2,1)S(1)}, bf16[18,352,128]{2,1,0:T(8,128)(2,1)}, u32[]{:S(2)}) copy-start(bf16[18,352,128]{2,1,0:T(8,128)(2,1)} %copy-done.4) | copy-start | bytes 4866052
  90.6 51.6 %all-to-all-start.1 = ((bf16[16,6,64,128]{3,2,1,0:T(8,128)(2,1)}), bf16[16,6,64,128]{3,2,1,0:T(8,128)(2,1)S(1)}, u32[]{:S(2)}, u32[]{:S(2)}) async-start(bf16[16,6,64,128]{3,2,1,0:T(8,128)(2,1)} %pack.3), calls=%async_computation.1 | async-start | bytes 3145728 | tf_op jit(solution)/shard_map/all_to_all | solution.py:457
  111.0 10.2 %copy-start = (bf16[18,256,384]{2,1,0:T(8,128)(2,1)S(1)}, bf16[18,256,384]{2,1,0:T(8,128)(2,1)}, u32[]{:S(2)}) copy-start(bf16[18,256,384]{2,1,0:T(8,128)(2,1)} %slice.123.act) | copy-start | bytes 10616836
  142.2 10.7 %copy-start.1 = (bf16[18,96,384]{2,1,0:T(8,128)(2,1)S(1)}, bf16[18,96,384]{2,1,0:T(8,128)(2,1)}, u32[]{:S(2)}) copy-start(bf16[18,96,384]{2,1,0:T(8,128)(2,1)} %slice.124.act) | copy-start | bytes 3981316
  148.0 6.2 %collective-permute-start.1 = (bf16[1,352,128]{2,1,0:T(8,128)(2,1)S(1)}, bf16[1,352,128]{2,1,0:T(8,128)(2,1)S(1)}, u32[]{:S(2)}, u32[]{:S(2)}) collective-permute-start(bf16[1,352,128]{2,1,0:T(8,128)(2,1)S(1)} %get-tuple-element.90), channel_id=1, source_target_pairs={{1,2},{3,4},{5,6},{7,8},{9,10},{11,12},{13,14},{2,1},{4,3},{6,5},{... | collective-permute-start | bytes 270344 | tf_op jit(solution)/shard_map/ppermute | solution.py:473
  148.8 5.4 %copy-start.2 = (bf16[2,352,384]{2,1,0:T(8,128)(2,1)S(1)}, bf16[2,352,384]{2,1,0:T(8,128)(2,1)}, u32[]{:S(2)}) copy-start(bf16[2,352,384]{2,1,0:T(8,128)(2,1)} %fusion.14.act) | copy-start | bytes 1622020
  148.8 5.4 %collective-permute-start = (bf16[1,352,128]{2,1,0:T(8,128)(2,1)S(1)}, bf16[1,352,128]{2,1,0:T(8,128)(2,1)S(1)}, u32[]{:S(2)}, u32[]{:S(2)}) collective-permute-start(bf16[1,352,128]{2,1,0:T(8,128)(2,1)S(1)} %get-tuple-element.91), channel_id=1, source_target_pairs={{0,1},{1,0},{2,3},{3,2},{4,5},{5,4},{6,7},{7,6},{8,9},{9,8},{10,11... | collective-permute-start | bytes 270344 | tf_op jit(solution)/shard_map/ppermute | solution.py:466
  154.8 2.1 %collective-permute-start.2 = (f32[832,128]{1,0:T(8,128)S(1)}, f32[832,128]{1,0:T(8,128)S(1)}, u32[]{:S(2)}, u32[]{:S(2)}) collective-permute-start(f32[832,128]{1,0:T(8,128)S(1)} %slice_select_fusion), channel_id=1, source_target_pairs={{0,1},{1,0},{2,3},{3,2},{4,5},{5,4},{6,7},{7,6},{8,9},{9,8},{10,11... | collective-permute-start | bytes 1277960 | tf_op jit(solution)/shard_map/ppermute | solution.py:466
  158.1 22.2 %all-to-all-start.2 = ((bf16[8,104,128]{2,1,0:T(8,128)(2,1)}), bf16[8,104,128]{2,1,0:T(8,128)(2,1)S(1)}, u32[]{:S(2)}, u32[]{:S(2)}) async-start(bf16[8,104,128]{2,1,0:T(8,128)(2,1)} %bitcast.7), calls=%async_computation.2 | async-start | bytes 425984 | tf_op jit(solution)/shard_map/all_to_all | solution.py:462
  178.8 1.4 collective-permute-start.3
  196.5 1.6 collective-permute-start.4

commit v4 on v3

--- a/solution.py
+++ b/solution.py
@@ -27,8 +27,12 @@
     return lax.dot_general(a, b, dims(1, 1), preferred_element_type=F32)
 
 
-def unit(count, offset, cap):
-    return max(u for u in range(1, cap + 1) if count % u == 0 and offset % u == 0)
+def mm_tn(a, b):
+    return lax.dot_general(a, b, dims(0, 0), preferred_element_type=F32)
+
+
+def unit(count, cap):
+    return max(u for u in range(1, cap + 1) if count % u == 0)
 
 
 def params():
@@ -48,6 +52,13 @@
 def whole(shape):
     zeros = (0,) * len(shape)
     return pl.BlockSpec(shape, lambda i: zeros)
+
+
+def at_columns(rows, units, channels, start):
+    return pl.BlockSpec(
+        (pl.Element(rows), pl.Element(units * BLK), pl.Element(channels)),
+        lambda i: (0, pl.multiple_of((start + i * units) * BLK, BLK), 0),
+    )
 
 
 def eye(size):
@@ -102,7 +113,7 @@
     depth = groups * LANES
     height = x.shape[1]
     side = 256 if height % 256 == 0 else LANES
-    u = unit(blocks, 0, 2)
+    u = unit(blocks, 2)
     steps = blocks // u
     anywhere = lambda: pl.BlockSpec(memory_space=pltpu.HBM)
     return pl.pallas_call(
@@ -172,7 +183,7 @@
     inner = mm_nt(masked, weight[...])
     sg[...] = jnp.where(pre > 0, inner, 0.0).astype(BF).reshape(sg.shape)
     act = jnp.maximum(pre, 0.0).astype(BF)
-    part = mm(jnp.transpose(act), masked)
+    part = mm_tn(act, masked)
     for t in range(tiles):
         lw[t] += part[:, t * LANES : (t + 1) * LANES]
 
@@ -181,10 +192,9 @@
     rows, _, channels = opre.shape
     count, blocks, height, _ = recv.shape
     tiles = channels // LANES
-    u = unit(blocks, start, 4)
-    first = start // u
+    u = unit(blocks, 4)
     alias = buf is not None
-    wide = lambda c: pl.BlockSpec((rows, u * BLK, c), lambda i: (0, first + i, 0))
+    wide = lambda c: at_columns(rows, u, c, start)
     pixels = rows * BLK * blocks
     call = pl.pallas_call(
         functools.partial(open_kernel, u, join, alias),
@@ -239,7 +249,7 @@
 def middle(sg, act, start):
     rows, width, _ = sg.shape
     blocks = width // BLK
-    u = unit(blocks, 0, 4)
+    u = unit(blocks, 4)
     return pl.pallas_call(
         functools.partial(middle_kernel, u),
         grid=(blocks // u,),
@@ -267,10 +277,10 @@
             top = (3 * a + b) * LANES
             out[top : top + LANES, :] = jnp.transpose(
                 sums[a][:, b * LANES : (b + 1) * LANES]
-            )
+            ).astype(BF)
     for t in range(lw.shape[0]):
         top = (9 + t) * LANES
-        out[top : top + LANES, :] = lw[t]
+        out[top : top + LANES, :] = lw[t].astype(BF)
 
 
 def add_rims(mw, lw, before, after, act):
@@ -279,7 +289,7 @@
         rim_kernel,
         in_specs=[space] * 5,
         out_specs=space,
-        out_shape=jax.ShapeDtypeStruct(((9 + lw.shape[0]) * LANES, LANES), F32),
+        out_shape=jax.ShapeDtypeStruct(((9 + lw.shape[0]) * LANES, LANES), BF),
         compiler_params=params(),
         cost_estimate=cost(2**20, 2**20),
         name="add_rims",
@@ -292,7 +302,7 @@
         part = mm(moved[2 - a], taps[a])
         acc = part if acc is None else acc + part
     grad = jnp.where(fpre.astype(F32) > 0, acc, 0.0).astype(BF)
-    total[...] += mm(jnp.transpose(grad), binput)
+    total[...] += mm_tn(grad, binput)
     return (mm_nt(grad, weight) + direct.astype(F32)).astype(BF)
 
 
@@ -306,8 +316,10 @@
         fw[...] = fw_in[...]
 
     inside = slice(1, 1 + rows)
+    width = units * BLK
+    cols = pl.ds(pl.multiple_of(pl.program_id(0) * width, width), width)
     out = add_pixels(
-        [sg[e : e + rows].reshape(pixels, 3 * LANES) for e in range(3)],
+        [sg[e : e + rows, cols, :].reshape(pixels, 3 * LANES) for e in range(3)],
         taps,
         fpre[inside].reshape(pixels, LANES),
         binput[inside].reshape(pixels, channels),
@@ -324,16 +336,15 @@
     rows, _, channels = binput.shape
     width = sg.shape[1]
     blocks = width // BLK
-    u = unit(blocks, start, 3)
-    first = start // u
-    wide = lambda c: pl.BlockSpec((rows, u * BLK, c), lambda i: (0, first + i, 0))
+    u = unit(blocks, 4)
+    wide = lambda c: at_columns(rows, u, c, start)
     pixels = rows * width
     return pl.pallas_call(
         functools.partial(close_kernel, u),
         grid=(blocks // u,),
         in_specs=[
             wide(channels),
-            pl.BlockSpec((sg.shape[0], u * BLK, 3 * LANES), lambda i: (0, i, 0)),
+            pl.BlockSpec(memory_space=pltpu.VMEM),
             whole(taps.shape),
             wide(LANES),
             wide(channels),
@@ -363,7 +374,7 @@
         total[...] = fw_in[...]
 
     buf[0] = add_pixels(
-        [sg[0, e] for e in range(3)],
+        [sg[step, e] for e in range(3)],
         taps,
         fpre[0],
         binput[0],
@@ -377,7 +388,7 @@
         for t in range(binput.shape[2] // LANES):
             fw[t * LANES : (t + 1) * LANES, :] = jnp.transpose(
                 total[:, t * LANES : (t + 1) * LANES]
-            )
+            ).astype(BF)
 
 
 def close_edges(buf, sg, taps, fpre, binput, weight, fw_in):
@@ -389,7 +400,7 @@
         grid=(2,),
         in_specs=[
             flat(channels),
-            pl.BlockSpec((1, 3, width, 3 * LANES), lambda i: (i, 0, 0, 0)),
+            pl.BlockSpec(memory_space=pltpu.VMEM),
             whole(taps.shape),
             flat(LANES),
             flat(channels),
@@ -399,7 +410,7 @@
         out_specs=[flat(channels), whole((channels, LANES))],
         out_shape=[
             jax.ShapeDtypeStruct(buf.shape, BF),
-            jax.ShapeDtypeStruct((channels, LANES), F32),
+            jax.ShapeDtypeStruct((channels, LANES), BF),
         ],
         scratch_shapes=[pltpu.VMEM(fw_in.shape, F32)],
         input_output_aliases={0: 0},
@@ -419,7 +430,7 @@
         for k in range(chips):
             a, b = mine[k, :size, :].astype(F32), other[k, :size, :].astype(F32)
             value = jnp.where(odd, a if h else b, b if h else a)
-            start = (h * chips + k) * size
+            start = (2 * k + h) * size
             at = start
             while at < start + size:
                 stop = min(start + size, (at // LANES + 1) * LANES)
@@ -430,14 +441,19 @@
                     t, m = divmod(at - top, LANES)
                     lw[m : m + stop - at, t * LANES : (t + 1) * LANES] = piece
                 at = stop
-    total = mine[0, size:, :].astype(F32)
-    for k in range(1, chips):
-        total = total + mine[k, size:, :].astype(F32)
-    fw[...] = total * factor
+    own = fw.shape[0]
+    sums = []
+    for c in range(2):
+        rows = slice(size + c * own, size + (c + 1) * own)
+        total = mine[0, rows, :].astype(F32) + other[0, rows, :].astype(F32)
+        for k in range(1, chips):
+            total += mine[k, rows, :].astype(F32) + other[k, rows, :].astype(F32)
+        sums.append(total)
+    fw[...] = jnp.where(odd, sums[1], sums[0]) * factor
 
 
 def finish(odd, mine, other, size, factor, inner, channels):
-    own = mine.shape[1] - size
+    own = (mine.shape[1] - size) // 2
     space = lambda: pl.BlockSpec(memory_space=pltpu.VMEM)
     return pl.pallas_call(
         functools.partial(finish_kernel, size, factor),
@@ -571,14 +587,11 @@
     mw = middle(sg_b, act_b, mw)
     both = add_rims(mw, lw, before[0], after[0], rim_act)
 
-    odd = lax.axis_index(AXIS) % 2 == 1
-    half = both.shape[0] // 2
-    size = half // (count // 2)
-    pair = (both[:half], both[half:])
-    kept, given = jnp.where(odd, pair[1], pair[0]), jnp.where(odd, pair[0], pair[1])
-    part = (kept + swap_cores(given, count)).astype(BF).reshape(-1, size, LANES)
-    part, fw, sg_b = lax.optimization_barrier((part, fw, sg_b))
-    parts = exchange_chips(part, count).astype(F32)
+    size = both.shape[0] // count
+    part, fw, sg_b = lax.optimization_barrier(
+        (both.reshape(count, size, LANES), fw, sg_b)
+    )
+    parts = exchange(part).astype(F32)
     share = (jnp.sum(parts, axis=0) * factor).astype(BF)
 
     far = jnp.concatenate([sg_a[:, seam - 1 :], sg_b], axis=1)
@@ -606,15 +619,20 @@
         first_weight,
         fw,
     )
-    fw = fw.reshape(count // 2, 2, own, LANES)
-    kept, given = jnp.where(odd, fw[:, 1], fw[:, 0]), jnp.where(odd, fw[:, 0], fw[:, 1])
-    fw = (kept + swap_cores(given, count)).astype(BF)
+    chips = count // 2
     got = exchange_chips(
-        jnp.concatenate([jnp.broadcast_to(share[None], part.shape), fw], axis=1), count
+        jnp.concatenate(
+            [
+                jnp.broadcast_to(share[None], (chips, size, LANES)),
+                fw.reshape(chips, 2 * own, LANES),
+            ],
+            axis=1,
+        ),
+        count,
     )
     other = swap_cores(got, count)
     middle_wgrad, last_wgrad, first_wgrad = finish(
-        odd.astype(jnp.int32).reshape(1), got, other, size, factor, inner, channels
+        (lax.axis_index(AXIS) % 2).reshape(1), got, other, size, factor, inner, channels
     )
     return (buf, first_wgrad, middle_wgrad.reshape(3, 3, inner, inner), last_wgrad)
 

time: 200 us -> 196 us (0.980)
    all_to_all x2 -> x3, starting transfers between devices: 27.2 us -> 36.3 us  [exchange(): return lax.all_to_all(value, AXIS, 0, 0, tiled=True)]
    all_to_all x1 -> x0, starting transfers between devices: 8.78 us -> none  [exchange_chips(): lax.all_to_all(value, AXIS, 0, 0, tiled=True, axis_index_groups=same_core)]
    ppermute x4 -> x2, waiting for transfers between devices: 4.21 us -> 1.65 us  [swap_cores(): return lax.ppermute(value, AXIS, [(i, i ^ 1) for i in range(count)])]
    all_to_all x2 -> x3, waiting for transfers between devices: 70.8 us -> 72.7 us  [exchange(): return lax.all_to_all(value, AXIS, 0, 0, tiled=True)]
    ppermute x4 -> x2, starting transfers between devices: 4.88 us -> 4.1 us  [swap_cores(): return lax.ppermute(value, AXIS, [(i, i ^ 1) for i in range(count)])]
  transfers between devices with their start and end apart: 8 -> 6, of which waited for: 5 -> 4; matrix products, arithmetic and copies ran while one was open for 7% -> 7% of each run, Pallas kernels for 19% -> 19%
where the time goes in v4:
time: 196 us; the launch traced here: 195 us
  waiting for transfers between devices  74.4 us (38%)
  Pallas kernels  48.4 us (25%)
  starting transfers between devices  41.2 us (21%)
  blocking collectives  15.3 us (8%)
  local copies, waits for them, and re-layouts  9.41 us (5%)
  other arithmetic  5.79 us (3%)
    all_to_all x3, waiting for transfers between devices, exchange(): return lax.all_to_all(value, AXIS, 0, 0, tiled=True)  72.7 us
    all_to_all x3, starting transfers between devices, exchange(): return lax.all_to_all(value, AXIS, 0, 0, tiled=True)  36.3 us
    pallas_call x2, Pallas kernels, open_block(): return call(*((buf,) + args if alias else args))  15.4 us
    all_to_all x1, blocking collectives, exchange_chips(): lax.all_to_all(value, AXIS, 0, 0, tiled=True, axis_index_groups=same_core)  15.3 us
    pallas_call x2, Pallas kernels, close_block(): pl.pallas_call(functools.partial(close_kernel, u), grid=(blocks // u,), i...  15.1 us
    pallas_call x2, Pallas kernels, pack(): pl.pallas_call(functools.partial(pack_kernel, tile_rows, groups, start),...  7.68 us
    pallas_call x2, Pallas kernels, middle(): pl.pallas_call(functools.partial(middle_kernel, u), grid=(blocks // u,),...  4.29 us
    ppermute x2, starting transfers between devices, swap_cores(): return lax.ppermute(value, AXIS, [(i, i ^ 1) for i in range(count)])  4.1 us
  transfers between devices with their start and end apart: 6, of which 4 were waited for; matrix products, arithmetic and copies ran while one was open for 7% of the time, Pallas kernels for 19%

profile of v4, /device:TPU:0, one launch (start us, length us, event | category | flops | bytes accessed | tf_op | source)
XLA Modules:
  0.0 195.4 jit_solution(8397467076036075007)
XLA Ops:
  0.7 4.7 %pack.2 = bf16[16,16,64,128]{3,2,1,0:T(8,128)(2,1)} custom-call(bf16[11264,256]{1,0:T(8,128)(2,1)} %bitcast.16, bf16[256,256]{1,0:T(8,128)(2,1)S(1)} %fusion.19.eye_ref), custom_call_target="tpu_custom_call" | custom-call | flops 16777216 | bytes 131072 | tf_op jit(solution)/shard_map/pack/pallas_call | solution.py:119
  5.3 7.6 %all-to-all-start = ((bf16[16,16,64,128]{3,2,1,0:T(8,128)(2,1)}), bf16[16,16,64,128]{3,2,1,0:T(8,128)(2,1)}, u32[]{:S(2)}, u32[]{:S(2)}) async-start(bf16[16,16,64,128]{3,2,1,0:T(8,128)(2,1)} %pack.2), calls=%async_computation | async-start | bytes 8388608 | tf_op jit(solution)/shard_map/all_to_all | solution.py:473
  15.2 1.2 slice.106.act
  16.4 2.3 %slice.105.act = bf16[18,256,384]{2,1,0:T(8,128)(2,1)} slice(bf16[18,352,384]{2,1,0:T(8,128)(2,1)S(1)} %pad_maximum_fusion), slice={[0:18], [0:256], [0:384]} | slice | bytes 7077888 | tf_op jit(solution)/shard_map/slice | solution.py:548
  18.7 1.8 copy.16
  20.6 3.0 %pack.3 = bf16[16,6,64,128]{3,2,1,0:T(8,128)(2,1)} custom-call(bf16[11264,256]{1,0:T(8,128)(2,1)} %bitcast.17, bf16[256,256]{1,0:T(8,128)(2,1)S(1)} %fusion.19.eye_ref), custom_call_target="tpu_custom_call" | custom-call | flops 6291456 | bytes 49152 | tf_op jit(solution)/shard_map/pack/pallas_call | solution.py:119
  25.3 1.0 fusion.7.refs_3_.refs_4_
  26.3 64.4 %all-to-all-done.refs_0_ = bf16[16,16,64,128]{3,2,1,0:T(8,128)(2,1)} async-done(((bf16[16,16,64,128]{3,2,1,0:T(8,128)(2,1)}), bf16[16,16,64,128]{3,2,1,0:T(8,128)(2,1)}, u32[]{:S(2)}, u32[]{:S(2)}) %all-to-all-start) | async-done | bytes 4194336 | tf_op jit(solution)/shard_map/all_to_all | solution.py:473
  90.6 19.6 %all-to-all-start.1 = ((bf16[16,6,64,128]{3,2,1,0:T(8,128)(2,1)}), bf16[16,6,64,128]{3,2,1,0:T(8,128)(2,1)S(1)}, u32[]{:S(2)}, u32[]{:S(2)}) async-start(bf16[16,6,64,128]{3,2,1,0:T(8,128)(2,1)} %pack.3), calls=%async_computation.1 | async-start | bytes 3145728 | tf_op jit(solution)/shard_map/all_to_all | solution.py:473
  111.0 10.2 %open_block.2 = (bf16[16,352,512]{2,1,0:T(8,128)(2,1)}, bf16[16,256,128]{2,1,0:T(8,128)(2,1)S(1)}, f32[4,128,128]{2,1,0:T(8,128)}) custom-call(bf16[16,16,64,128]{3,2,1,0:T(8,128)(2,1)} %all-to-all-done.refs_0_, bf16[16,352,512]{2,1,0:T(8,128)(2,1)} %refs_2_.3, bf16[16,352,128]{2,1,0:T(8,128)(2,1)} %refs_3_.1, bf16[512,512]{1,0:T(8,128)(2,1)} %fusion.7.refs_3_.refs_4_, ...), custom_call_target="tpu_custom_call" | custom-call | flops 67108864 | bytes 229376 | tf_op jit(solution)/shard_map/open_block/pallas_call | solution.py:232
  121.2 3.0 %middle.2.start_ref = f32[3,128,384]{2,1,0:T(8,128)S(1)} custom-call(bf16[16,256,128]{2,1,0:T(8,128)(2,1)S(1)} %get-tuple-element.43.sg, bf16[18,256,384]{2,1,0:T(8,128)(2,1)S(1)} %copy-done, f32[3,128,384]{2,1,0:T(8,128)S(1)} %broadcast_in_dim.9.start_ref), custom_call_target="tpu_custom_call" | custom-call | flops 18874368 | bytes 65536 | tf_op jit(solution)/shard_map/middle/pallas_call | solution.py:253
  125.9 9.9 %close_block.2 = (bf16[16,352,512]{2,1,0:T(8,128)(2,1)}, f32[128,512]{1,0:T(8,128)}) custom-call(bf16[16,352,512]{2,1,0:T(8,128)(2,1)} %get-tuple-element.42.buf_in, bf16[16,224,384]{2,1,0:T(8,128)(2,1)S(1)} %pad_maximum_fusion.1.sg, bf16[3,384,128]{2,1,0:T(8,128)(2,1)} %bitcast.18, bf16[16,352,128]{2,1,0:T(8,128)(2,1)} %fpre.2, ...), custom_call_target="tpu_custom_call", output_to_operand_aliasing={{0}: (0, {})} | custom-call | flops 31195136 | bytes 229376 | tf_op jit(solution)/shard_map/close_block/pallas_call | solution.py:342
  135.8 6.5 %all-to-all-done.1.refs_1_ = bf16[16,6,64,128]{3,2,1,0:T(8,128)(2,1)S(1)} async-done(((bf16[16,6,64,128]{3,2,1,0:T(8,128)(2,1)}), bf16[16,6,64,128]{3,2,1,0:T(8,128)(2,1)S(1)}, u32[]{:S(2)}, u32[]{:S(2)}) %all-to-all-start.1) | async-done | bytes 1572896 | tf_op jit(solution)/shard_map/all_to_all | solution.py:473
  142.2 5.3 %open_block.3 = (bf16[16,352,512]{2,1,0:T(8,128)(2,1)}, bf16[16,96,128]{2,1,0:T(8,128)(2,1)S(1)}, f32[4,128,128]{2,1,0:T(8,128)S(1)}) custom-call(bf16[16,352,512]{2,1,0:T(8,128)(2,1)} %get-tuple-element.46.refs_0_, bf16[16,6,64,128]{3,2,1,0:T(8,128)(2,1)S(1)} %all-to-all-done.1.refs_1_, ...), custom_call_target="tpu_custom_call", output_to_operand_aliasing={{0}: (0, {})} | custom-call | flops 25165824 | bytes 86016 | tf_op jit(solution)/shard_map/open_block/pallas_call | solution.py:232
  148.4 4.1 %collective-permute-start = (bf16[1,352,128]{2,1,0:T(8,128)(2,1)S(1)}, bf16[1,352,128]{2,1,0:T(8,128)(2,1)S(1)}, u32[]{:S(2)}, u32[]{:S(2)}) collective-permute-start(bf16[1,352,128]{2,1,0:T(8,128)(2,1)S(1)} %get-tuple-element.91), channel_id=1, source_target_pairs={{0,1},{1,0},{2,3},{3,2},{4,5},{5,4},{6,7},{7,6},{8,9},{9,8},{10,11... | collective-permute-start | bytes 270344 | tf_op jit(solution)/shard_map/ppermute | solution.py:482
  152.6 1.3 middle.3.mw
  154.0 1.2 add_rims.1
  155.6 9.0 %all-to-all-start.2 = ((bf16[16,104,128]{2,1,0:T(8,128)(2,1)}), bf16[16,104,128]{2,1,0:T(8,128)(2,1)S(1)}, u32[]{:S(2)}, u32[]{:S(2)}) async-start(bf16[16,104,128]{2,1,0:T(8,128)(2,1)} %bitcast.7), calls=%async_computation.2 | async-start | bytes 851968 | tf_op jit(solution)/shard_map/all_to_all | solution.py:473
  165.1 5.3 %close_block.3 = (bf16[16,352,512]{2,1,0:T(8,128)(2,1)}, f32[128,512]{1,0:T(8,128)}) custom-call(bf16[16,352,512]{2,1,0:T(8,128)(2,1)} %get-tuple-element.53.buf_in, bf16[16,128,384]{2,1,0:T(8,128)(2,1)S(1)} %pad_maximum_fusion.3.sg, bf16[3,384,128]{2,1,0:T(8,128)(2,1)} %bitcast.19, bf16[16,352,128]{2,1,0:T(8,128)(2,1)} %fpre.2, ...), custom_call_target="tpu_custom_call", output_to_operand_aliasing={{0}: (0, {})} | custom-call | flops 17825792 | bytes 131072 | tf_op jit(solution)/shard_map/close_block/pallas_call | solution.py:342
  170.7 1.0 pad_maximum_fusion.2
  171.8 3.7 %close_edges.1 = (bf16[16,352,512]{2,1,0:T(8,128)(2,1)}, bf16[512,128]{1,0:T(8,128)(2,1)S(1)}) custom-call(bf16[16,352,512]{2,1,0:T(8,128)(2,1)} %get-tuple-element.62.buf_in, bf16[2,3,352,384]{3,2,1,0:T(8,128)(2,1)S(1)} %bitcast.12, bf16[3,384,128]{2,1,0:T(8,128)(2,1)} %bitcast.20, bf16[16,352,128]{2,1,0:T(8,128)(2,1)} %fpre.2, ...), custom_call_target="tpu_custom_call", output_to_operand_aliasing={{0}: (0, {})} | custom-call | flops 6127616 | bytes 33792 | tf_op jit(solution)/shard_map/close_edges/pallas_call | solution.py:398
  175.5 1.9 all-to-all-done.2
  177.5 15.3 %all_to_all.20.mine = bf16[8,168,128]{2,1,0:T(8,128)(2,1)S(1)} all-to-all(bf16[8,168,128]{2,1,0:T(8,128)(2,1)S(1)} %pad_maximum_fusion.5), channel_id=1, replica_groups={{0,2,4,6,8,10,12,14},{1,3,5,7,9,11,13,15},{16,18,20,22,24,26,28,30},{17..., dimensions={0} | all-to-all | bytes 688128 | tf_op jit(solution)/shard_map/all_to_all | solution.py:478
  192.8 1.6 collective-permute-done.2.other
  (47 shorter events, 9.6 us)
Async XLA Ops:
  5.3 7.6 %copy-start.3 = (bf16[16,352,128]{2,1,0:T(8,128)(2,1)S(1)}, bf16[16,352,128]{2,1,0:T(8,128)(2,1)}, u32[]{:S(2)}) copy-start(bf16[16,352,128]{2,1,0:T(8,128)(2,1)} %fpre.2) | copy-start | bytes 4325380
  5.3 85.3 %all-to-all-start = ((bf16[16,16,64,128]{3,2,1,0:T(8,128)(2,1)}), bf16[16,16,64,128]{3,2,1,0:T(8,128)(2,1)}, u32[]{:S(2)}, u32[]{:S(2)}) async-start(bf16[16,16,64,128]{3,2,1,0:T(8,128)(2,1)} %pack.2), calls=%async_computation | async-start | bytes 8388608 | tf_op jit(solution)/shard_map/all_to_all | solution.py:473
  13.9 1.3 copy-start.4
  20.6 3.0 %copy-start.5 = (bf16[18,352,128]{2,1,0:T(8,128)(2,1)S(1)}, bf16[18,352,128]{2,1,0:T(8,128)(2,1)}, u32[]{:S(2)}) copy-start(bf16[18,352,128]{2,1,0:T(8,128)(2,1)} %copy-done.4) | copy-start | bytes 4866052
  90.6 51.6 %all-to-all-start.1 = ((bf16[16,6,64,128]{3,2,1,0:T(8,128)(2,1)}), bf16[16,6,64,128]{3,2,1,0:T(8,128)(2,1)S(1)}, u32[]{:S(2)}, u32[]{:S(2)}) async-start(bf16[16,6,64,128]{3,2,1,0:T(8,128)(2,1)} %pack.3), calls=%async_computation.1 | async-start | bytes 3145728 | tf_op jit(solution)/shard_map/all_to_all | solution.py:473
  111.0 10.2 %copy-start = (bf16[18,256,384]{2,1,0:T(8,128)(2,1)S(1)}, bf16[18,256,384]{2,1,0:T(8,128)(2,1)}, u32[]{:S(2)}) copy-start(bf16[18,256,384]{2,1,0:T(8,128)(2,1)} %slice.105.act) | copy-start | bytes 10616836
  142.2 10.4 %copy-start.1 = (bf16[18,96,384]{2,1,0:T(8,128)(2,1)S(1)}, bf16[18,96,384]{2,1,0:T(8,128)(2,1)}, u32[]{:S(2)}) copy-start(bf16[18,96,384]{2,1,0:T(8,128)(2,1)} %slice.106.act) | copy-start | bytes 3981316
  147.6 6.4 %collective-permute-start.1 = (bf16[1,352,128]{2,1,0:T(8,128)(2,1)S(1)}, bf16[1,352,128]{2,1,0:T(8,128)(2,1)S(1)}, u32[]{:S(2)}, u32[]{:S(2)}) collective-permute-start(bf16[1,352,128]{2,1,0:T(8,128)(2,1)S(1)} %get-tuple-element.90), channel_id=1, source_target_pairs={{1,2},{3,4},{5,6},{7,8},{9,10},{11,12},{13,14},{2,1},{4,3},{6,5},{... | collective-permute-start | bytes 270344 | tf_op jit(solution)/shard_map/ppermute | solution.py:489
  148.4 5.5 %collective-permute-start = (bf16[1,352,128]{2,1,0:T(8,128)(2,1)S(1)}, bf16[1,352,128]{2,1,0:T(8,128)(2,1)S(1)}, u32[]{:S(2)}, u32[]{:S(2)}) collective-permute-start(bf16[1,352,128]{2,1,0:T(8,128)(2,1)S(1)} %get-tuple-element.91), channel_id=1, source_target_pairs={{0,1},{1,0},{2,3},{3,2},{4,5},{5,4},{6,7},{7,6},{8,9},{9,8},{10,11... | collective-permute-start | bytes 270344 | tf_op jit(solution)/shard_map/ppermute | solution.py:482
  152.6 1.4 copy-start.2
  155.6 21.8 %all-to-all-start.2 = ((bf16[16,104,128]{2,1,0:T(8,128)(2,1)}), bf16[16,104,128]{2,1,0:T(8,128)(2,1)S(1)}, u32[]{:S(2)}, u32[]{:S(2)}) async-start(bf16[16,104,128]{2,1,0:T(8,128)(2,1)} %bitcast.7), calls=%async_computation.2 | async-start | bytes 851968 | tf_op jit(solution)/shard_map/all_to_all | solution.py:473
  192.8 1.7 collective-permute-start.2

commit v5 on v4

--- a/solution.py
+++ b/solution.py
@@ -36,7 +36,7 @@
 
 
 def params():
-    return pltpu.CompilerParams(vmem_limit_bytes=24 * 2**20)
+    return pltpu.CompilerParams(vmem_limit_bytes=32 * 2**20)
 
 
 def hbm(value):
@@ -113,7 +113,7 @@
     depth = groups * LANES
     height = x.shape[1]
     side = 256 if height % 256 == 0 else LANES
-    u = unit(blocks, 2)
+    u = unit(blocks, 4)
     steps = blocks // u
     anywhere = lambda: pl.BlockSpec(memory_space=pltpu.HBM)
     return pl.pallas_call(
@@ -192,7 +192,7 @@
     rows, _, channels = opre.shape
     count, blocks, height, _ = recv.shape
     tiles = channels // LANES
-    u = unit(blocks, 4)
+    u = unit(blocks, 6)
     alias = buf is not None
     wide = lambda c: at_columns(rows, u, c, start)
     pixels = rows * BLK * blocks
@@ -336,7 +336,7 @@
     rows, _, channels = binput.shape
     width = sg.shape[1]
     blocks = width // BLK
-    u = unit(blocks, 4)
+    u = unit(blocks, 7)
     wide = lambda c: at_columns(rows, u, c, start)
     pixels = rows * width
     return pl.pallas_call(
@@ -519,10 +519,10 @@
     join = LANES // own
     groups = BLK // join
     blocks = map_cols // BLK
-    head = 4 * (3 * blocks // 16)
+    head = blocks - 4
     tail = blocks - head
     split = head * BLK
-    closed = head - 2
+    closed = head - 4
     seam = closed * BLK
 
     turned = jnp.transpose(output_grad, (1, 2, 0)).reshape(map_cols * own, -1)

time: 196 us -> 195 us (level)
  waiting for transfers between devices: 74.4 us -> 79.1 us
  Pallas kernels: 48.4 us -> 44.9 us
    all_to_all x3, waiting for transfers between devices: 72.7 us -> 77.4 us  [exchange(): return lax.all_to_all(value, AXIS, 0, 0, tiled=True)]
    ppermute x2, starting transfers between devices: 4.1 us -> 0.45 us  [swap_cores(): return lax.ppermute(value, AXIS, [(i, i ^ 1) for i in range(count)])]
    all_to_all x3, starting transfers between devices: 36.3 us -> 39.4 us  [exchange(): return lax.all_to_all(value, AXIS, 0, 0, tiled=True)]
    pallas_call x2, Pallas kernels: 15.1 us -> 12.5 us  [close_block(): pl.pallas_call(functools.partial(close_kernel, u), grid=(blocks // u,), i...]
  transfers between devices with their start and end apart: 6 -> 6, of which waited for: 4 -> 3; matrix products, arithmetic and copies ran while one was open for 7% -> 6% of each run, Pallas kernels for 19% -> 18%
where the time goes in v5:
time: 195 us; the launch traced here: 194 us
  waiting for transfers between devices  79.1 us (41%)
  Pallas kernels  44.9 us (23%)
  starting transfers between devices  40.5 us (21%)
  blocking collectives  15 us (8%)
  local copies, waits for them, and re-layouts  8.19 us (4%)
  other arithmetic  5.7 us (3%)
    all_to_all x3, waiting for transfers between devices, exchange(): return lax.all_to_all(value, AXIS, 0, 0, tiled=True)  77.4 us
    all_to_all x3, starting transfers between devices, exchange(): return lax.all_to_all(value, AXIS, 0, 0, tiled=True)  39.4 us
    all_to_all x1, blocking collectives, exchange_chips(): lax.all_to_all(value, AXIS, 0, 0, tiled=True, axis_index_groups=same_core)  15 us
    pallas_call x2, Pallas kernels, open_block(): return call(*((buf,) + args if alias else args))  14.8 us
    pallas_call x2, Pallas kernels, close_block(): pl.pallas_call(functools.partial(close_kernel, u), grid=(blocks // u,), i...  12.5 us
    pallas_call x2, Pallas kernels, pack(): pl.pallas_call(functools.partial(pack_kernel, tile_rows, groups, start),...  7.45 us
    pallas_call x2, Pallas kernels, middle(): pl.pallas_call(functools.partial(middle_kernel, u), grid=(blocks // u,),...  4.29 us
  transfers between devices with their start and end apart: 6, of which 3 were waited for; matrix products, arithmetic and copies ran while one was open for 6% of the time, Pallas kernels for 18%

profile of v5, /device:TPU:0, one launch (start us, length us, event | category | flops | bytes accessed | tf_op | source)
XLA Modules:
  0.0 194.4 jit_solution(917880495516189617)
XLA Ops:
  0.7 4.5 %pack.2 = bf16[16,18,64,128]{3,2,1,0:T(8,128)(2,1)} custom-call(bf16[11264,256]{1,0:T(8,128)(2,1)} %bitcast.16, bf16[256,256]{1,0:T(8,128)(2,1)S(1)} %fusion.19.eye_ref), custom_call_target="tpu_custom_call" | custom-call | flops 18874368 | bytes 147456 | tf_op jit(solution)/shard_map/pack/pallas_call | solution.py:119
  5.2 7.6 %all-to-all-start = ((bf16[16,18,64,128]{3,2,1,0:T(8,128)(2,1)}), bf16[16,18,64,128]{3,2,1,0:T(8,128)(2,1)}, u32[]{:S(2)}, u32[]{:S(2)}) async-start(bf16[16,18,64,128]{3,2,1,0:T(8,128)(2,1)} %pack.2), calls=%async_computation | async-start | bytes 9437184 | tf_op jit(solution)/shard_map/all_to_all | solution.py:473
  12.9 0.9 pad_slice_fusion.2
  15.5 2.3 %slice.105.act = bf16[18,288,384]{2,1,0:T(8,128)(2,1)} slice(bf16[18,352,384]{2,1,0:T(8,128)(2,1)S(1)} %pad_maximum_fusion), slice={[0:18], [0:288], [0:384]} | slice | bytes 7962624 | tf_op jit(solution)/shard_map/slice | solution.py:548
  17.8 0.9 copy.16
  18.7 2.9 %pack.3 = bf16[16,4,64,128]{3,2,1,0:T(8,128)(2,1)} custom-call(bf16[11264,256]{1,0:T(8,128)(2,1)} %bitcast.17, bf16[256,256]{1,0:T(8,128)(2,1)S(1)} %fusion.19.eye_ref), custom_call_target="tpu_custom_call" | custom-call | flops 4194304 | bytes 32768 | tf_op jit(solution)/shard_map/pack/pallas_call | solution.py:119
  21.8 0.9 fusion.14.act
  22.7 0.8 fusion.20.refs_4_.refs_5_
  23.4 0.9 fusion.7.refs_3_.refs_4_
  24.4 75.2 %all-to-all-done.refs_0_ = bf16[16,18,64,128]{3,2,1,0:T(8,128)(2,1)} async-done(((bf16[16,18,64,128]{3,2,1,0:T(8,128)(2,1)}), bf16[16,18,64,128]{3,2,1,0:T(8,128)(2,1)}, u32[]{:S(2)}, u32[]{:S(2)}) %all-to-all-start) | async-done | bytes 4718624 | tf_op jit(solution)/shard_map/all_to_all | solution.py:473
  99.6 21.8 %all-to-all-start.1 = ((bf16[16,4,64,128]{3,2,1,0:T(8,128)(2,1)}), bf16[16,4,64,128]{3,2,1,0:T(8,128)(2,1)S(1)}, u32[]{:S(2)}, u32[]{:S(2)}) async-start(bf16[16,4,64,128]{3,2,1,0:T(8,128)(2,1)} %pack.3), calls=%async_computation.1 | async-start | bytes 2097152 | tf_op jit(solution)/shard_map/all_to_all | solution.py:473
  122.1 10.6 %open_block.2 = (bf16[16,352,512]{2,1,0:T(8,128)(2,1)}, bf16[16,288,128]{2,1,0:T(8,128)(2,1)S(1)}, f32[4,128,128]{2,1,0:T(8,128)}) custom-call(bf16[16,18,64,128]{3,2,1,0:T(8,128)(2,1)} %all-to-all-done.refs_0_, bf16[16,352,512]{2,1,0:T(8,128)(2,1)} %refs_2_.3, bf16[16,352,128]{2,1,0:T(8,128)(2,1)} %refs_3_.1, bf16[512,512]{1,0:T(8,128)(2,1)} %fusion.7.refs_3_.refs_4_, ...), custom_call_target="tpu_custom_call" | custom-call | flops 75497472 | bytes 258048 | tf_op jit(solution)/shard_map/open_block/pallas_call | solution.py:232
  132.8 3.7 %middle.2.start_ref = f32[3,128,384]{2,1,0:T(8,128)S(1)} custom-call(bf16[16,288,128]{2,1,0:T(8,128)(2,1)S(1)} %get-tuple-element.43.sg, bf16[18,288,384]{2,1,0:T(8,128)(2,1)S(1)} %copy-done, f32[3,128,384]{2,1,0:T(8,128)S(1)} %broadcast_in_dim.9.start_ref), custom_call_target="tpu_custom_call" | custom-call | flops 21233664 | bytes 73728 | tf_op jit(solution)/shard_map/middle/pallas_call | solution.py:253
  138.4 7.2 %close_block.2 = (bf16[16,352,512]{2,1,0:T(8,128)(2,1)}, f32[128,512]{1,0:T(8,128)}) custom-call(bf16[16,352,512]{2,1,0:T(8,128)(2,1)} %get-tuple-element.42.buf_in, bf16[16,224,384]{2,1,0:T(8,128)(2,1)S(1)} %pad_maximum_fusion.1.sg, bf16[3,384,128]{2,1,0:T(8,128)(2,1)} %bitcast.18, bf16[16,352,128]{2,1,0:T(8,128)(2,1)} %fpre.2, ...), custom_call_target="tpu_custom_call", output_to_operand_aliasing={{0}: (0, {})} | custom-call | flops 31195136 | bytes 229376 | tf_op jit(solution)/shard_map/close_block/pallas_call | solution.py:342
  145.6 4.2 %open_block.3 = (bf16[16,352,512]{2,1,0:T(8,128)(2,1)}, bf16[16,64,128]{2,1,0:T(8,128)(2,1)S(1)}, f32[4,128,128]{2,1,0:T(8,128)S(1)}) custom-call(bf16[16,352,512]{2,1,0:T(8,128)(2,1)} %get-tuple-element.46.refs_0_, bf16[16,4,64,128]{3,2,1,0:T(8,128)(2,1)S(1)} %all-to-all-done.1.refs_1_, ...), custom_call_target="tpu_custom_call", output_to_operand_aliasing={{0}: (0, {})} | custom-call | flops 16777216 | bytes 57344 | tf_op jit(solution)/shard_map/open_block/pallas_call | solution.py:232
  152.1 1.2 add_rims.1
  153.8 10.0 %all-to-all-start.2 = ((bf16[16,104,128]{2,1,0:T(8,128)(2,1)}), bf16[16,104,128]{2,1,0:T(8,128)(2,1)S(1)}, u32[]{:S(2)}, u32[]{:S(2)}) async-start(bf16[16,104,128]{2,1,0:T(8,128)(2,1)} %bitcast.7), calls=%async_computation.2 | async-start | bytes 851968 | tf_op jit(solution)/shard_map/all_to_all | solution.py:473
  164.1 5.3 %close_block.3 = (bf16[16,352,512]{2,1,0:T(8,128)(2,1)}, f32[128,512]{1,0:T(8,128)}) custom-call(bf16[16,352,512]{2,1,0:T(8,128)(2,1)} %get-tuple-element.53.buf_in, bf16[16,128,384]{2,1,0:T(8,128)(2,1)S(1)} %pad_maximum_fusion.3.sg, bf16[3,384,128]{2,1,0:T(8,128)(2,1)} %bitcast.19, bf16[16,352,128]{2,1,0:T(8,128)(2,1)} %fpre.2, ...), custom_call_target="tpu_custom_call", output_to_operand_aliasing={{0}: (0, {})} | custom-call | flops 17825792 | bytes 131072 | tf_op jit(solution)/shard_map/close_block/pallas_call | solution.py:342
  169.8 0.9 pad_maximum_fusion.2
  170.7 3.7 %close_edges.1 = (bf16[16,352,512]{2,1,0:T(8,128)(2,1)}, bf16[512,128]{1,0:T(8,128)(2,1)S(1)}) custom-call(bf16[16,352,512]{2,1,0:T(8,128)(2,1)} %get-tuple-element.62.buf_in, bf16[2,3,352,384]{3,2,1,0:T(8,128)(2,1)S(1)} %bitcast.12, bf16[3,384,128]{2,1,0:T(8,128)(2,1)} %bitcast.20, bf16[16,352,128]{2,1,0:T(8,128)(2,1)} %fpre.2, ...), custom_call_target="tpu_custom_call", output_to_operand_aliasing={{0}: (0, {})} | custom-call | flops 6127616 | bytes 33792 | tf_op jit(solution)/shard_map/close_edges/pallas_call | solution.py:398
  174.4 2.2 %all-to-all-done.2 = bf16[16,104,128]{2,1,0:T(8,128)(2,1)S(1)} async-done(((bf16[16,104,128]{2,1,0:T(8,128)(2,1)}), bf16[16,104,128]{2,1,0:T(8,128)(2,1)S(1)}, u32[]{:S(2)}, u32[]{:S(2)}) %all-to-all-start.2) | async-done | bytes 426016 | tf_op jit(solution)/shard_map/all_to_all | solution.py:473
  176.7 15.0 %all_to_all.20.mine = bf16[8,168,128]{2,1,0:T(8,128)(2,1)S(1)} all-to-all(bf16[8,168,128]{2,1,0:T(8,128)(2,1)S(1)} %pad_maximum_fusion.6), channel_id=1, replica_groups={{0,2,4,6,8,10,12,14},{1,3,5,7,9,11,13,15},{16,18,20,22,24,26,28,30},{17..., dimensions={0} | all-to-all | bytes 688128 | tf_op jit(solution)/shard_map/all_to_all | solution.py:478
  191.8 1.6 collective-permute-done.2.other
  193.4 0.9 finish.1
  (55 shorter events, 8.0 us)
Async XLA Ops:
  5.2 7.6 %copy-start.8 = (bf16[16,352,128]{2,1,0:T(8,128)(2,1)S(1)}, bf16[16,352,128]{2,1,0:T(8,128)(2,1)}, u32[]{:S(2)}) copy-start(bf16[16,352,128]{2,1,0:T(8,128)(2,1)} %fpre.2) | copy-start | bytes 4325380
  5.2 94.4 %all-to-all-start = ((bf16[16,18,64,128]{3,2,1,0:T(8,128)(2,1)}), bf16[16,18,64,128]{3,2,1,0:T(8,128)(2,1)}, u32[]{:S(2)}, u32[]{:S(2)}) async-start(bf16[16,18,64,128]{3,2,1,0:T(8,128)(2,1)} %pack.2), calls=%async_computation | async-start | bytes 9437184 | tf_op jit(solution)/shard_map/all_to_all | solution.py:473
  13.8 1.1 copy-start.4
  13.8 1.6 copy-start.6
  15.5 2.3 %copy-start.9 = (bf16[3,3,128,128]{3,2,1,0:T(8,128)(2,1)S(1)}, bf16[3,3,128,128]{3,2,1,0:T(8,128)(2,1)}, u32[]{:S(2)}) copy-start(bf16[3,3,128,128]{3,2,1,0:T(8,128)(2,1)} %param.14) | copy-start | bytes 884740
  18.7 2.9 %copy-start.5 = (bf16[18,352,128]{2,1,0:T(8,128)(2,1)S(1)}, bf16[18,352,128]{2,1,0:T(8,128)(2,1)}, u32[]{:S(2)}) copy-start(bf16[18,352,128]{2,1,0:T(8,128)(2,1)} %copy-done.4) | copy-start | bytes 4866052
  18.7 3.0 %copy-start.7 = (bf16[18,352,128]{2,1,0:T(8,128)(2,1)S(1)}, bf16[18,352,128]{2,1,0:T(8,128)(2,1)}, u32[]{:S(2)}) copy-start(bf16[18,352,128]{2,1,0:T(8,128)(2,1)} %copy-done.6) | copy-start | bytes 4866052
  99.6 46.0 %all-to-all-start.1 = ((bf16[16,4,64,128]{3,2,1,0:T(8,128)(2,1)}), bf16[16,4,64,128]{3,2,1,0:T(8,128)(2,1)S(1)}, u32[]{:S(2)}, u32[]{:S(2)}) async-start(bf16[16,4,64,128]{3,2,1,0:T(8,128)(2,1)} %pack.3), calls=%async_computation.1 | async-start | bytes 2097152 | tf_op jit(solution)/shard_map/all_to_all | solution.py:473
  122.1 10.6 %copy-start = (bf16[18,288,384]{2,1,0:T(8,128)(2,1)S(1)}, bf16[18,288,384]{2,1,0:T(8,128)(2,1)}, u32[]{:S(2)}) copy-start(bf16[18,288,384]{2,1,0:T(8,128)(2,1)} %slice.105.act) | copy-start | bytes 11943940
  136.5 0.8 copy-start.1
  149.8 1.3 copy-start.2
  149.9 1.9 collective-permute-start
  150.3 1.4 collective-permute-start.1
  151.0 1.0 copy-start.3
  153.8 22.8 %all-to-all-start.2 = ((bf16[16,104,128]{2,1,0:T(8,128)(2,1)}), bf16[16,104,128]{2,1,0:T(8,128)(2,1)S(1)}, u32[]{:S(2)}, u32[]{:S(2)}) async-start(bf16[16,104,128]{2,1,0:T(8,128)(2,1)} %bitcast.7), calls=%async_computation.2 | async-start | bytes 851968 | tf_op jit(solution)/shard_map/all_to_all | solution.py:473
  191.8 1.7 collective-permute-start.2
